TPU v7x, 32 devices: a whole 2x2x4 slice. The times are simulated.
32 devices in a mesh: row: 4 (over y, x), col: 8 (over z, core).
Axes of the slice: x: 2, y: 2, z: 4, core: 2. Of those that a mesh axis runs over, the one named last changes fastest.
Arguments:
- spectra: bfloat16 [8192, 2, 8, 256], P(('row', 'col')), may hold values from -6 to 6
- pair_grad: bfloat16 [4, 2048, 2, 8, 8192], P(None, 'col', None, None, 'row'), may hold values from -0.0625 to 0.0625
- assign: int32 [8192], replicated, may hold values from 0 to 8191, each once
- tile_mask: int32 [128, 128], replicated, may hold values 0 or 1
Outputs:
- spectra_grad: float32 [8192, 2, 8, 256], P(('row', 'col'))
Inputs may be any that keep to these rules, and one draw needn't show every extreme that they name: `assign`: each number of 0 to 8191 appears once.
All inputs are finite; a program needn't handle non-finite values.
Results may differ from a plain program's by a relative error of at most 0.0003.
Values may be sent and summed in bfloat16 or wider, within the bound.
A program may use at most 384 MiB of HBM per device.

v0:
```python
from functools import partial

import jax
import jax.numpy as jnp
from jax import lax
from jax.sharding import PartitionSpec as P

TILE = 64


def body(spectra, pair_grad, assign, tile_mask):
    row_index = lax.axis_index("row")
    col_index = lax.axis_index("col")
    blocks, width_b, _, bins, block_p = pair_grad.shape
    row_spec = lax.all_gather(spectra, "col", axis=0, tiled=True)
    col_spec = lax.all_gather(spectra, "row", axis=0, tiled=True)
    p_places = row_index * block_p + jnp.arange(block_p, dtype=jnp.int32)
    q_places = (
        jnp.arange(blocks, dtype=jnp.int32)[:, None] * block_p
        + col_index * width_b
        + jnp.arange(width_b, dtype=jnp.int32)[None, :]
    ).reshape(-1)
    p_owner = lax.dynamic_slice_in_dim(assign, row_index * block_p, block_p)
    q_owner = jnp.take(assign, q_places)
    mask_flipped = tile_mask.T
    tile_q = jnp.take(mask_flipped, q_places // TILE, axis=0)
    tile_grid = jnp.take(tile_q, p_places // TILE, axis=1)
    counted = (tile_grid == 1) & (p_owner[None, :] <= q_owner[:, None])
    grads = pair_grad.reshape(blocks * width_b, 2, bins, block_p)
    masked = jnp.where(counted[:, None, None, :], grads, jnp.zeros((), jnp.bfloat16))
    real_g = masked[:, 0]
    imag_g = masked[:, 1]
    col_real = col_spec[:, 0]
    col_imag = col_spec[:, 1]
    row_real = row_spec[:, 0]
    row_imag = row_spec[:, 1]
    to_rows = partial(jnp.einsum, "qfp,qfw->pfw", preferred_element_type=jnp.float32)
    to_columns = partial(jnp.einsum, "qfp,pfw->qfw", preferred_element_type=jnp.float32)
    real_s = real_g
    imag_s = imag_g
    part_real = to_rows(real_s, col_real) - to_rows(imag_s, col_imag)
    part_imag = to_rows(real_s, col_imag) + to_rows(imag_s, col_real)
    summed = lax.psum_scatter(
        jnp.stack([part_real, part_imag], axis=1), "col", scatter_dimension=0, tiled=True
    )
    real_s = real_g
    imag_s = imag_g
    part_real = to_columns(real_s, row_real) + to_columns(imag_s, row_imag)
    part_imag = to_columns(real_s, row_imag) - to_columns(imag_s, row_real)
    column_summed = lax.psum_scatter(
        jnp.stack([part_real, part_imag], axis=1), "row", scatter_dimension=0, tiled=True
    )
    return summed + column_summed


def solution(mesh):
    return jax.shard_map(
        body,
        mesh=mesh,
        in_specs=(P(("row", "col"), None, None, None), P(None, "col", None, None, "row"), P(), P()),
        out_specs=P(("row", "col"), None, None, None),
        check_vma=False,
    )
```

profile of v0, /device:TPU:24, one launch (start us, length us, event | category | flops | bytes accessed | tf_op | source)
XLA Modules:
  0.0 762.0 jit_solution(8850664690631640267)
XLA Ops:
  6.5 0.0 all-gather.5.cloned.1.call-start
  6.5 3.6 copy.18
  10.2 0.0 all-gather.5.cloned.1.call-update
  10.2 0.0 all-gather.3.cloned.1.call-start
  10.2 0.7 all-gather.3.cloned.1.call-update
  10.9 0.0 reduce-scatter.5.cloned.1.call-start
  11.0 0.1 compare_select_fusion
  11.1 0.1 fusion.15
  11.3 5.8 gather_fusion.2
  17.1 0.9 copy.15
  18.0 2.8 gather_fusion
  20.9 0.2 broadcast_select_fusion.1
  21.1 0.2 copy.16
  21.3 90.0 %copy.29 = bf16[1024,2,8,2048]{0,3,2,1:T(8,128)(2,1)} copy(bf16[1024,2,8,2048]{3,2,1,0:T(8,128)(2,1)} %bitcast.5) | data formatting | bytes 134217728 | tf_op jit(solution)/shard_map/reshape | solution.py:29
  111.3 0.0 dynamic-slice-start
  111.3 9.8 %gather_fusion.1 = s32[2048,1024]{1,0:T(8,128)} fusion(s32[1024,128]{0,1:T(8,128)S(1)} %copy.16, s32[2048]{0:T(1024)S(1)} %broadcast_clamp_fusion), kind=kCustom, calls=%fused_computation.1 | custom fusion | bytes 16785408 | tf_op jit(solution)/shard_map/jit(_take)/gather | solution.py:27
  121.1 0.0 dynamic-slice-done
  121.1 4.5 fusion.9
  125.7 44.7 %broadcast_select_fusion = bf16[1024,2,8,2048]{0,3,2,1:T(8,128)(2,1)} fusion(bf16[1024,2,8,2048]{0,3,2,1:T(8,128)(2,1)} %copy.29, pred[1024,2048]{0,1:T(8,128)(4,1)S(1)} %fusion.9), kind=kLoop, calls=%fused_computation.3 | loop fusion | flops 33554432 | bytes 136314880 | tf_op jit(solution)/shard_map/jit(_where)/select_n | solution.py:30
  170.4 0.0 all-gather.5.cloned.1.call-done
  170.4 21.2 %fusion.1 = f32[8,1024,256]{2,1,0:T(8,128)} fusion(bf16[1024,2,8,2048]{0,3,2,1:T(8,128)(2,1)} %broadcast_select_fusion, bf16[2048,2,8,256]{3,0,2,1:T(8,128)(2,1)} %all-gather.5.cloned.1.call-done), kind=kOutput, calls=%fused_computation.8 | convolution fusion | flops 8589934592 | bytes 50331648 | tf_op jit(solution)/shard_map/qfp,pfw->qfw/dot_general | solution.py:48
  191.7 22.5 %add_bitcast_fusion.1 = f32[1024,1,8,256]{3,0,2,1:T(8,128)} fusion(f32[8,1024,256]{2,1,0:T(8,128)} %fusion.1, bf16[2048,2,8,256]{3,0,2,1:T(8,128)(2,1)} %all-gather.5.cloned.1.call-done, bf16[1024,2,8,2048]{0,3,2,1:T(8,128)(2,1)} %broadcast_select_fusion), kind=kOutput, calls=%fused_computation.22 | convolution fusion | flops 8592031744 | bytes 58720256 | tf_op jit(solution)/shard_map/qfp,pfw->qfw/dot_general | solution.py:48
  214.2 19.9 %fusion = f32[8,1024,256]{2,1,0:T(8,128)} fusion(bf16[1024,2,8,2048]{0,3,2,1:T(8,128)(2,1)} %broadcast_select_fusion, bf16[2048,2,8,256]{3,0,2,1:T(8,128)(2,1)} %all-gather.5.cloned.1.call-done), kind=kOutput, calls=%fused_computation.7 | convolution fusion | flops 8589934592 | bytes 50331648 | tf_op jit(solution)/shard_map/qfp,pfw->qfw/dot_general | solution.py:49
  234.0 21.7 %subtract_bitcast_fusion.1 = f32[1024,1,8,256]{3,0,2,1:T(8,128)} fusion(f32[8,1024,256]{2,1,0:T(8,128)} %fusion, bf16[2048,2,8,256]{3,0,2,1:T(8,128)(2,1)} %all-gather.5.cloned.1.call-done, bf16[1024,2,8,2048]{0,3,2,1:T(8,128)(2,1)} %broadcast_select_fusion), kind=kOutput, calls=%fused_computation.21 | convolution fusion | flops 8592031744 | bytes 58720256 | tf_op jit(solution)/shard_map/qfp,pfw->qfw/dot_general | solution.py:49
  255.8 11.5 %pad_maximum_fusion.1 = f32[1024,2,8,256]{3,0,2,1:T(8,128)} fusion(f32[1024,1,8,256]{3,0,2,1:T(8,128)} %subtract_bitcast_fusion.1, f32[1024,1,8,256]{3,0,2,1:T(8,128)} %add_bitcast_fusion.1), kind=kLoop, calls=%fused_computation.15 | loop fusion | flops 4194304 | bytes 33554432 | tf_op jit(solution)/shard_map/stack | solution.py:51
  267.3 0.0 reduce-scatter.5.cloned.1.call-update
  267.3 0.0 reduce-scatter.3.cloned.1.call-start
  267.4 0.0 all-gather.3.cloned.1.call-done
  267.4 22.5 %fusion.2 = f32[8,2048,256]{2,1,0:T(8,128)} fusion(bf16[1024,2,8,2048]{0,3,2,1:T(8,128)(2,1)} %broadcast_select_fusion, bf16[1024,2,8,256]{3,0,2,1:T(8,128)(2,1)} %all-gather.3.cloned.1.call-done), kind=kOutput, calls=%fused_computation.9 | convolution fusion | flops 8589934592 | bytes 54525952 | tf_op jit(solution)/shard_map/qfp,qfw->pfw/dot_general | solution.py:42
  289.9 23.1 %fusion.3 = f32[8,2048,256]{2,1,0:T(8,128)} fusion(bf16[1024,2,8,2048]{0,3,2,1:T(8,128)(2,1)} %broadcast_select_fusion, bf16[1024,2,8,256]{3,0,2,1:T(8,128)(2,1)} %all-gather.3.cloned.1.call-done), kind=kOutput, calls=%fused_computation.10 | convolution fusion | flops 8589934592 | bytes 54525952 | tf_op jit(solution)/shard_map/qfp,qfw->pfw/dot_general | solution.py:41
  313.0 26.7 %add_bitcast_fusion = f32[2048,1,8,256]{3,0,2,1:T(8,128)} fusion(f32[8,2048,256]{2,1,0:T(8,128)} %fusion.2, bf16[1024,2,8,2048]{0,3,2,1:T(8,128)(2,1)} %broadcast_select_fusion, bf16[1024,2,8,256]{3,0,2,1:T(8,128)(2,1)} %all-gather.3.cloned.1.call-done), kind=kOutput, calls=%fused_computation.16 | convolution fusion | flops 8594128896 | bytes 71303168 | tf_op jit(solution)/shard_map/qfp,qfw->pfw/dot_general | solution.py:42
  339.7 26.9 %subtract_bitcast_fusion = f32[2048,1,8,256]{3,0,2,1:T(8,128)} fusion(f32[8,2048,256]{2,1,0:T(8,128)} %fusion.3, bf16[1024,2,8,2048]{0,3,2,1:T(8,128)(2,1)} %broadcast_select_fusion, bf16[1024,2,8,256]{3,0,2,1:T(8,128)(2,1)} %all-gather.3.cloned.1.call-done), kind=kOutput, calls=%fused_computation.17 | convolution fusion | flops 8594128896 | bytes 71303168 | tf_op jit(solution)/shard_map/qfp,qfw->pfw/dot_general | solution.py:41
  366.5 23.0 %pad_maximum_fusion = f32[2048,2,8,256]{3,0,2,1:T(8,128)} fusion(f32[2048,1,8,256]{3,0,2,1:T(8,128)} %add_bitcast_fusion, f32[2048,1,8,256]{3,0,2,1:T(8,128)} %subtract_bitcast_fusion), kind=kLoop, calls=%fused_computation.6 | loop fusion | flops 8388608 | bytes 67108864 | tf_op jit(solution)/shard_map/stack | solution.py:44
  389.5 0.0 reduce-scatter.3.cloned.1.call-update
  389.6 32.2 %reduce-scatter.5.cloned.1.call-done = f32[256,2,8,256]{3,0,2,1:T(8,128)} async-done(((f32[1024,2,8,256]{3,0,2,1:T(8,128)}), f32[256,2,8,256]{3,0,2,1:T(8,128)}) %reduce-scatter.5.cloned.1.call-update) | async-done | bytes 4194320 | tf_op jit(solution)/shard_map/reduce_scatter | solution.py:50
  421.8 325.2 %reduce-scatter.3.cloned.1.call-done = f32[256,2,8,256]{3,0,2,1:T(8,128)} async-done(((f32[2048,2,8,256]{3,0,2,1:T(8,128)}), f32[256,2,8,256]{3,0,2,1:T(8,128)}) %reduce-scatter.3.cloned.1.call-update) | async-done | bytes 4194320 | tf_op jit(solution)/shard_map/reduce_scatter | solution.py:43
  747.0 4.0 add.204
  751.1 4.4 copy.24
  (10 shorter events, 0.1 us)
Async XLA Ops:
  6.5 163.9 %all-gather.5.cloned.1.call-start = ((), (), s32[]{:S(2)}) async-start(), calls=%async_computation.4 | async-start | bytes 18874368 | tf_op jit(solution)/shard_map/all_gather | solution.py:15
  10.2 257.2 %all-gather.3.cloned.1.call-start = ((), (), s32[]{:S(2)}) async-start(), calls=%async_computation.2 | async-start | bytes 10485760 | tf_op jit(solution)/shard_map/all_gather | solution.py:16
  10.9 410.8 %reduce-scatter.5.cloned.1.call-start = ((), (), s32[]{:S(2)}) async-start(), calls=%async_computation.5 | async-start | bytes 20971520 | tf_op jit(solution)/shard_map/reduce_scatter | solution.py:50
  111.3 9.9 %dynamic-slice-start = ((s32[8192]{0:T(1024)}, s32[]{:T(128)}), s32[2048]{0:T(1024)S(1)}, s32[]{:S(2)}) async-start(s32[8192]{0:T(1024)} %param.6, s32[]{:T(128)} %select_n.117), calls=%async_computation.6 | async-start | bytes 16896 | tf_op jit(solution)/shard_map/dynamic_slice | solution.py:23
  267.3 479.7 %reduce-scatter.3.cloned.1.call-start = ((), (), s32[]{:S(2)}) async-start(), calls=%async_computation.3 | async-start | bytes 37748736 | tf_op jit(solution)/shard_map/reduce_scatter | solution.py:43
Sparse Core Ops, SparseCore 0:
  10.3 149.0 all-gather.4
  161.2 88.8 all-gather.2
  267.4 154.3 reduce-scatter.4
  424.0 322.9 reduce-scatter.2
where the time goes:
time: 769 us; the launch traced here: 762 us
  waiting for transfers between devices  358 us (47%)
  matrix products  184 us (24%)
  local copies, waits for them, and re-layouts  118 us (15%)
  other arithmetic  88.2 us (11%)
  between operations  13.3 us (2%)
    reduce_scatter x1, waiting for transfers between devices, body(): lax.psum_scatter(jnp.stack([part_real, part_imag], axis=1), 'col', scatte...  325 us
    reshape x1, local copies, waits for them, and re-layouts, body(): grads = pair_grad.reshape(blocks * width_b, 2, bins, block_p)  90 us
    dot_general x2, matrix products, body(): part_real = to_rows(real_s, col_real) - to_rows(imag_s, col_imag)  50 us
    dot_general x2, matrix products, body(): part_imag = to_rows(real_s, col_imag) + to_rows(imag_s, col_real)  49.2 us
    select_n x1, other arithmetic, body(): jnp.where(counted[:, None, None, :], grads, jnp.zeros((), jnp.bfloat16))  44.7 us
    dot_general x2, matrix products, body(): part_real = to_columns(real_s, row_real) + to_columns(imag_s, row_imag)  43.8 us
    dot_general x2, matrix products, body(): part_imag = to_columns(real_s, row_imag) - to_columns(imag_s, row_real)  41.6 us
    another operation x2, other arithmetic, body(): jnp.stack([part_real, part_imag], axis=1)  34.5 us
  transfers between devices with their start and end apart: 4, of which 2 were waited for; matrix products, arithmetic and copies ran while one was open for 50% of the time, Pallas kernels for 0%

commit v1 on v0

v1 whole, which is shorter than its diff:
```python
import jax
import jax.numpy as jnp
from jax import lax
from jax.experimental.layout import Layout, with_layout_constraint
from jax.sharding import PartitionSpec as P

TILE = 64
CHUNKS = 2
SCALE = 8.0


def pick(x, index, axis):
    return lax.dynamic_index_in_dim(x, index, axis, keepdims=False)


def swap_cores(x, n_col):
    return lax.ppermute(x, "col", [(i, i ^ 1) for i in range(n_col)])


def line_perm(sources, step, n_col):
    line = n_col // 2
    return [
        (z * 2 + core, (z + step) * 2 + core)
        for z in sources
        for core in range(2)
        if 0 <= z + step < line
    ]


def major(x):
    return with_layout_constraint(x, Layout(major_to_minor=tuple(range(x.ndim))))


def both(spec, sign):
    width = spec.shape[-1] // 2
    one, none = jnp.eye(width, dtype=spec.dtype), jnp.zeros((width, width), spec.dtype)
    same = jnp.block([[one, none], [none, one]])
    turn = jnp.block([[none, sign * one], [-sign * one, none]]).astype(spec.dtype)
    return jnp.einsum("fin,cnm->cfim", spec, jnp.stack([same, turn]), preferred_element_type=spec.dtype)


def gather_line(block, z, core, n_col):
    line = n_col // 2
    to_right, to_left = [block], [block]
    for step in range(line - 1):
        to_right.append(lax.ppermute(to_right[-1], "col", line_perm(range(step, line), 1, n_col)))
        to_left.append(lax.ppermute(to_left[-1], "col", line_perm(range(line - step), -1, n_col)))
    held = major(jnp.zeros(block.shape[:1] + (n_col,) + block.shape[1:], block.dtype))
    for step in range(line):
        got = block if step == 0 else jnp.where(z >= step, to_right[step], to_left[line - step])
        source = lax.rem(z - step + line, line) * 2
        held = lax.dynamic_update_slice(held, got[:, None], (0, source + core, 0, 0))
        other = swap_cores(got, n_col)
        held = lax.dynamic_update_slice(held, other[:, None], (0, source + 1 - core, 0, 0))
    return major(held).reshape(block.shape[0], -1, block.shape[-1])


def gather_cube(block, row, n_row, bits):
    parts = [(0, block)]
    for bit in bits:
        perm = [(i, i ^ (1 << bit)) for i in range(n_row)]
        parts = parts + [(far | (1 << bit), lax.ppermute(x, "row", perm)) for far, x in parts]
    held = major(jnp.zeros(block.shape[:1] + (n_row,) + block.shape[1:], block.dtype))
    for far, x in parts:
        held = lax.dynamic_update_slice(held, x[:, None], (0, row ^ far, 0, 0))
    return major(held).reshape(block.shape[0], -1, block.shape[-1])


def after(x, *others):
    return lax.optimization_barrier((x,) + others)


class LineSum:
    def __init__(self, part, z, core, n_col):
        bins, rows, cols = part.shape
        self.z, self.core, self.n_col, self.line = z, core, n_col, n_col // 2
        part = part.reshape(bins, self.line, 2, rows // n_col, cols)
        self.keep = pick(part, core, 2)
        self.swapped = swap_cores(pick(part, 1 - core, 2), n_col)
        self.right = self.left = None
        self.step = 0

    def encode(self):
        if self.step == 0:
            self.chip = self.keep + self.swapped
        self.step += 1
        right = pick(self.chip, jnp.clip(self.line - self.step + self.z, 0, self.line - 1), 1)
        left = pick(self.chip, jnp.clip(self.step - self.line + self.z, 0, self.line - 1), 1)
        if self.step > 1:
            right, left = right + self.right, left + self.left
        self.out = [(x * SCALE).astype(jnp.float16) for x in (right, left)]

    def send(self):
        line, step, n_col = self.line, self.step, self.n_col
        right = lax.ppermute(self.out[0], "col", line_perm(range(step), 1, n_col))
        left = lax.ppermute(self.out[1], "col", line_perm(range(line - step, line), -1, n_col))
        self.right, self.left = [x.astype(jnp.float32) * (1.0 / SCALE) for x in (right, left)]

    def total(self):
        while self.step < self.line - 1:
            self.encode()
            self.send()
        return pick(self.chip, self.z, 1) + self.right + self.left


def reduce_cube(part, row, n_row, bits):
    bins, rows, cols = part.shape
    part = part.reshape((bins,) + (2,) * len(bits) + (rows // n_row, cols))
    left = sorted(bits, reverse=True)
    for bit in bits:
        axis = 1 + left.index(bit)
        high = (row >> bit) & 1
        perm = [(i, i ^ (1 << bit)) for i in range(n_row)]
        part = pick(part, high, axis) + lax.ppermute(pick(part, 1 - high, axis), "row", perm)
        left.remove(bit)
    return part


def make_body(n_row, n_col):
    def body(spectra, pair_grad, assign, tile_mask):
        row = lax.axis_index("row")
        col = lax.axis_index("col")
        z, core = col // 2, col % 2
        blocks, width_b, _, bins, block_p = pair_grad.shape
        cube_bits = list(range(n_row.bit_length() - 1))
        per = bins // CHUNKS
        own = jnp.concatenate([jnp.swapaxes(spectra[:, d], 0, 1) for d in range(2)], axis=-1)
        pieces = [major(own[k * per : (k + 1) * per]) for k in range(CHUNKS)]
        orders = [cube_bits[:: (-1) ** k] for k in range(CHUNKS)]
        col_specs = [gather_cube(x, row, n_row, bits) for x, bits in zip(pieces, orders)]
        row_specs = [gather_line(x, z, core, n_col) for x in pieces]

        p_owner = lax.dynamic_slice_in_dim(assign, row * block_p, block_p)
        q_owner = pick(assign.reshape(blocks, n_col, width_b), col, 1).reshape(-1)
        tiles = lax.dynamic_slice_in_dim(tile_mask, row * (block_p // TILE), block_p // TILE, axis=0)
        tiles = pick(tiles.reshape(block_p // TILE, blocks, n_col, width_b // TILE), col, 2)
        tiles = tiles.reshape(block_p // TILE, -1).T
        grid = jnp.repeat(jnp.repeat(tiles, TILE, axis=1), TILE, axis=0)
        counted = (grid == 1) & (p_owner[None, :] <= q_owner[:, None])

        grads = pair_grad.reshape(blocks * width_b, 2, bins, block_p)
        grads = jnp.transpose(grads, (1, 2, 0, 3))
        masked = [
            jnp.where(counted, grads[:, k * per : (k + 1) * per], jnp.zeros((), jnp.bfloat16))
            for k in range(CHUNKS)
        ]
        sums = []
        for k in range(CHUNKS):
            row_part = jnp.einsum(
                "cfqp,cfqn->fpn", masked[k], both(col_specs[k], 1), preferred_element_type=jnp.float32
            )
            sums.append(LineSum(row_part, z, core, n_col))
        outs = []
        for k in range(CHUNKS):
            ready = []
            for line_sum in sums[: k + 1]:
                if line_sum.step < line_sum.line - 1:
                    line_sum.encode()
                    ready.append(line_sum)
            sent = [x for line_sum in ready for x in line_sum.out]
            spec, *sent = after(row_specs[k], *sent)
            for i, line_sum in enumerate(ready):
                line_sum.out = sent[2 * i : 2 * i + 2]
                line_sum.send()
            col_part = jnp.einsum(
                "cfqp,cfpn->fqn", masked[k], both(spec, -1), preferred_element_type=jnp.float32
            )
            outs.append(reduce_cube(col_part, row, n_row, orders[k]))
        totals = [x + line_sum.total() for x, line_sum in zip(outs, sums)]
        width = spectra.shape[3]
        halves = [
            jnp.concatenate([x[:, :, d * width : (d + 1) * width] for x in totals], axis=0) for d in range(2)
        ]
        return jnp.transpose(major(jnp.stack(halves, axis=0)), (2, 0, 1, 3))

    return body


def solution(mesh):
    return jax.shard_map(
        make_body(mesh.shape["row"], mesh.shape["col"]),
        mesh=mesh,
        in_specs=(P(("row", "col"), None, None, None), P(None, "col", None, None, "row"), P(), P()),
        out_specs=P(("row", "col"), None, None, None),
        check_vma=False,
    )
```

time: 769 us -> 612 us (0.80)
  waiting for transfers between devices: 358 us -> 132 us
  starting transfers between devices: 0.12 us -> 79.6 us
  local copies, waits for them, and re-layouts: 118 us -> 153 us
  matrix products: 184 us -> 154 us
  between operations: 13.3 us -> 1.07 us
    reduce_scatter x2 -> x0, waiting for transfers between devices: 357 us -> none  [the longest x1 325 us: body(): lax.psum_scatter(jnp.stack([part_real, part_imag], axis=1), 'col', scatte...]
    ppermute x0 -> x44, waiting for transfers between devices: none -> 132 us  [the longest x6 61.4 us: gather_line(): lax.ppermute(to_right[-1], 'col', line_perm(range(step, line), 1, n_col))]
    ppermute x0 -> x44, starting transfers between devices: none -> 79.6 us  [the longest x6 39.2 us: send(): lax.ppermute(self.out[1], 'col', line_perm(range(line - step, line), -1,...]
    select_n x5 -> x0, other arithmetic: 45 us -> none  [the longest x1 44.7 us: body(): jnp.where(counted[:, None, None, :], grads, jnp.zeros((), jnp.bfloat16))]
    dynamic_slice x2 -> x10, local copies, waits for them, and re-layouts: 0.01 us -> 37.2 us  [the longest x7 37.2 us: pick(): return lax.dynamic_index_in_dim(x, index, axis, keepdims=False)]
    add x2 -> x6, other arithmetic: 4.05 us -> 37.8 us  [the longest x2 23.1 us: encode(): self.chip = self.keep + self.swapped]
    another operation x2 -> x3, other arithmetic: 34.5 us -> 1.24 us  [the longest x1 0.92 us: both(): jnp.stack([same, turn])]
    reshape x1, local copies, waits for them, and re-layouts: 90 us -> 57.2 us  [body(): grads = pair_grad.reshape(blocks * width_b, 2, bins, block_p)]
  transfers between devices with their start and end apart: 4 -> 44, of which waited for: 2 -> 12; matrix products, arithmetic and copies ran while one was open for 50% -> 62% of each run, Pallas kernels for 0% -> 0%
where the time goes in v1:
time: 612 us; the launch traced here: 602 us
  matrix products  154 us (25%)
  local copies, waits for them, and re-layouts  153 us (25%)
  waiting for transfers between devices  132 us (22%)
  other arithmetic  82.6 us (13%)
  starting transfers between devices  79.6 us (13%)
    ppermute x6, waiting for transfers between devices, gather_line(): lax.ppermute(to_right[-1], 'col', line_perm(range(step, line), 1, n_col))  61.4 us
    dot_general x2, matrix products, body(): jnp.einsum('cfqp,cfpn->fqn', masked[k], both(spec, -1), preferred_element...  57.4 us
    reshape x1, local copies, waits for them, and re-layouts, body(): grads = pair_grad.reshape(blocks * width_b, 2, bins, block_p)  57.2 us
    dot_general x2, matrix products, body(): jnp.einsum('cfqp,cfqn->fpn', masked[k], both(col_specs[k], 1), preferred_...  53.1 us
    dot_general x4, matrix products, both(): jnp.einsum('fin,cnm->cfim', spec, jnp.stack([same, turn]), preferred_elem...  43.4 us
    ppermute x6, waiting for transfers between devices, send(): lax.ppermute(self.out[1], 'col', line_perm(range(line - step, line), -1,...  41.5 us
    ppermute x6, starting transfers between devices, send(): lax.ppermute(self.out[1], 'col', line_perm(range(line - step, line), -1,...  39.2 us
    dynamic_slice x7, local copies, waits for them, and re-layouts, pick(): return lax.dynamic_index_in_dim(x, index, axis, keepdims=False)  37.2 us
  transfers between devices with their start and end apart: 44, of which 12 were waited for; matrix products, arithmetic and copies ran while one was open for 62% of the time, Pallas kernels for 0%

profile of v1, /device:TPU:24, one launch (start us, length us, event | category | flops | bytes accessed | tf_op | source)
XLA Modules:
  0.0 602.4 jit_solution(9493845772742921753)
XLA Ops:
  10.0 57.2 %copy.92 = bf16[1024,2,8,2048]{3,0,1,2:T(8,128)(2,1)} copy(bf16[1024,2,8,2048]{3,2,1,0:T(8,128)(2,1)} %bitcast.5) | data formatting | bytes 134217728 | tf_op jit(solution)/shard_map/reshape | solution.py:141
  67.3 2.8 bitcast_and_fusion
  73.8 4.3 broadcast.55.clone.1
  79.2 4.3 broadcast.55.clone
  84.5 2.8 bitcast_dynamic-update-slice_fusion
  90.0 4.6 collective-permute-start.18
  107.0 9.7 %collective-permute-done.1 = bf16[4,256,512]{2,1,0:T(8,128)(2,1)} collective-permute-done((bf16[4,256,512]{2,1,0:T(8,128)(2,1)S(1)}, bf16[4,256,512]{2,1,0:T(8,128)(2,1)}, u32[]{:S(2)}, u32[]{:S(2)}) %collective-permute-start.1) | collective-permute-done | bytes 1048608 | tf_op jit(solution)/shard_map/ppermute | solution.py:46
  120.3 18.9 %collective-permute-done.17 = bf16[4,256,512]{2,1,0:T(8,128)(2,1)} collective-permute-done((bf16[4,256,512]{2,1,0:T(8,128)(2,1)S(1)}, bf16[4,256,512]{2,1,0:T(8,128)(2,1)}, u32[]{:S(2)}, u32[]{:S(2)}) %collective-permute-start.17) | collective-permute-done | bytes 1048608 | tf_op jit(solution)/shard_map/ppermute | solution.py:46
  143.9 6.6 %fusion.139 = bf16[2,4,1024,512]{3,2,0,1:T(8,128)(2,1)} fusion(bf16[4,1024,512,1]{2,1,3,0:T(8,128)(2,1)S(1)} %bitcast.341, bf16[1,512,512]{2,1,0:T(8,128)(2,1)S(1)} %get-tuple-element.62, bf16[1,512,512]{2,1,0:T(8,128)(2,1)S(1)} %get-tuple-element.63), kind=kOutput, calls=%fused_computation.24.clone.2 | convolution fusion | flops 4297064448 | bytes 13631488 | tf_op jit(solution)/shard_map/fin,cnm->cfim/dot_general | solution.py:39
  152.3 26.6 %fusion.1 = f32[4,2048,512,1]{2,1,3,0:T(8,128)} fusion(bf16[2,8,1024,2048]{3,2,0,1:T(8,128)(2,1)} %bitcast.332, pred[1024,2048]{1,0:T(8,128)(4,1)S(1)} %copy-done.11, bf16[2,4,1024,512]{3,2,0,1:T(8,128)(2,1)} %fusion.139), kind=kOutput, calls=%fused_computation.4 | convolution fusion | flops 17196646400 | bytes 60817408 | tf_op jit(solution)/shard_map/cfqp,cfqn->fpn/dot_general | solution.py:149
  181.2 2.7 bitcast_dynamic-update-slice_fusion.12
  186.9 6.6 %fusion.147 = bf16[2,4,1024,512]{3,2,0,1:T(8,128)(2,1)} fusion(bf16[4,1024,512,1]{2,1,3,0:T(8,128)(2,1)S(1)} %bitcast.342, bf16[1,512,512]{2,1,0:T(8,128)(2,1)S(1)} %copy-done.20, bf16[1,512,512]{2,1,0:T(8,128)(2,1)S(1)} %copy-done.22), kind=kOutput, calls=%fused_computation.23.clone.2 | convolution fusion | flops 4297064448 | bytes 13631488 | tf_op jit(solution)/shard_map/fin,cnm->cfim/dot_general | solution.py:39
  204.1 9.5 %constant_dynamic-slice_fusion.7 = (f32[4,4,1,256,512]{4,3,2,1,0:T(8,128)}, f32[4,4,1,256,512]{4,3,2,1,0:T(8,128)S(1)}) fusion(f32[4,4,2,256,512]{4,3,2,1,0:T(8,128)} %bitcast.337, s32[]{:T(128)S(6)} %select_n.179, s32[]{:T(128)S(6)} %select_n.180), kind=kLoop, calls=%fused_computation.136 | loop fusion | bytes 33554440 | tf_op jit(solution)/shard_map/jit(dynamic_index_in_dim)/dynamic_slice | solution.py:13
  213.7 4.3 copy.94
  219.1 13.7 %collective-permute-done.8 = bf16[4,256,512]{2,1,0:T(8,128)(2,1)S(1)} collective-permute-done((bf16[4,256,512]{2,1,0:T(8,128)(2,1)}, bf16[4,256,512]{2,1,0:T(8,128)(2,1)S(1)}, u32[]{:S(2)}, u32[]{:S(2)}) %collective-permute-start.8) | collective-permute-done | bytes 1048608 | tf_op jit(solution)/shard_map/ppermute | solution.py:46
  235.6 19.1 %collective-permute-done.24 = bf16[4,256,512]{2,1,0:T(8,128)(2,1)S(1)} collective-permute-done((bf16[4,256,512]{2,1,0:T(8,128)(2,1)}, bf16[4,256,512]{2,1,0:T(8,128)(2,1)S(1)}, u32[]{:S(2)}, u32[]{:S(2)}) %collective-permute-start.24) | collective-permute-done | bytes 1048608 | tf_op jit(solution)/shard_map/ppermute | solution.py:46
  256.0 26.6 %fusion.3 = f32[4,2048,512,1]{2,1,3,0:T(8,128)} fusion(bf16[2,8,1024,2048]{3,2,0,1:T(8,128)(2,1)} %bitcast.332, pred[1024,2048]{1,0:T(8,128)(4,1)S(1)} %copy-done.11, bf16[2,4,1024,512]{3,2,0,1:T(8,128)(2,1)} %fusion.147), kind=kOutput, calls=%fused_computation.6 | convolution fusion | flops 17196646400 | bytes 60817408 | tf_op jit(solution)/shard_map/cfqp,cfqn->fpn/dot_general | solution.py:149
  282.6 9.6 %constant_dynamic-slice_fusion.3 = (f32[4,4,1,256,512]{4,3,2,1,0:T(8,128)}, f32[4,4,1,256,512]{4,3,2,1,0:T(8,128)S(1)}) fusion(f32[4,4,2,256,512]{4,3,2,1,0:T(8,128)} %bitcast.338, s32[]{:T(128)S(6)} %select_n.179, s32[]{:T(128)S(6)} %select_n.180), kind=kLoop, calls=%fused_computation.132 | loop fusion | bytes 33554440 | tf_op jit(solution)/shard_map/jit(dynamic_index_in_dim)/dynamic_slice | solution.py:13
  292.1 4.4 copy.93
  301.6 11.5 %fusion.11 = f32[4,4,256,512]{3,2,0,1:T(8,128)} fusion(f32[4,4,256,512]{3,2,0,1:T(8,128)} %collective-permute-done.13, f32[4,4,1,256,512]{4,3,2,1,0:T(8,128)} %get-tuple-element.39), kind=kLoop, calls=%fused_computation.18 | loop fusion | flops 2097152 | bytes 25165824 | tf_op jit(solution)/shard_map/add | solution.py:85
  313.1 4.1 fusion.49
  318.0 2.6 collective-permute-start.27
  320.5 15.3 %fusion.135 = bf16[2,4,2048,512]{3,2,0,1:T(8,128)(2,1)} fusion(bf16[4,2048,512]{2,1,0:T(8,128)(2,1)} %bitcast.28, bf16[1,512,512]{2,1,0:T(8,128)(2,1)} %copy-done.19, bf16[1,512,512]{2,1,0:T(8,128)(2,1)} %get-tuple-element.61), kind=kOutput, calls=%fused_computation.8.clone.2 | convolution fusion | flops 8592031744 | bytes 26214400 | tf_op jit(solution)/shard_map/fin,cnm->cfim/dot_general | solution.py:39
  335.8 28.7 %fusion = f32[4,1024,512,1]{2,1,3,0:T(8,128)} fusion(bf16[2,8,1024,2048]{3,2,0,1:T(8,128)(2,1)} %bitcast.332, pred[1024,2048]{1,0:T(8,128)(4,1)S(1)} %copy-done.11, bf16[2,4,2048,512]{3,2,0,1:T(8,128)(2,1)} %fusion.135), kind=kOutput, calls=%fused_computation.3 | convolution fusion | flops 17196646400 | bytes 60817408 | tf_op jit(solution)/shard_map/cfqp,cfpn->fqn/dot_general | solution.py:165
  364.5 6.5 %constant_dynamic-slice_fusion.5 = (f32[4,2,1,256,512]{4,3,2,1,0:T(8,128)}, f32[4,2,1,256,512]{4,3,2,1,0:T(8,128)S(1)}) fusion(f32[4,2,2,256,512]{4,3,2,1,0:T(8,128)} %bitcast.340, s32[]{:T(128)S(6)} %select_n.181, s32[]{:T(128)S(6)} %select_n.182), kind=kLoop, calls=%fused_computation.134 | loop fusion | bytes 16777224 | tf_op jit(solution)/shard_map/jit(dynamic_index_in_dim)/dynamic_slice | solution.py:13
  375.1 11.6 %fusion.10 = f32[4,4,256,512]{3,2,0,1:T(8,128)} fusion(f32[4,4,256,512]{3,2,0,1:T(8,128)} %collective-permute-done.31, f32[4,4,1,256,512]{4,3,2,1,0:T(8,128)} %get-tuple-element.37), kind=kLoop, calls=%fused_computation.15 | loop fusion | flops 2097152 | bytes 25165824 | tf_op jit(solution)/shard_map/add | solution.py:85
  386.7 4.1 fusion.51
  391.8 4.6 fusion.39
  396.4 14.9 %fusion.143 = bf16[2,4,2048,512]{3,2,0,1:T(8,128)(2,1)} fusion(bf16[4,2048,512]{2,1,0:T(8,128)(2,1)} %bitcast.73, bf16[1,512,512]{2,1,0:T(8,128)(2,1)} %copy-done.19, bf16[1,512,512]{2,1,0:T(8,128)(2,1)} %get-tuple-element.61), kind=kOutput, calls=%fused_computation.7.clone.2 | convolution fusion | flops 8592031744 | bytes 26214400 | tf_op jit(solution)/shard_map/fin,cnm->cfim/dot_general | solution.py:39
  411.2 28.7 %fusion.2 = f32[4,1024,512,1]{2,1,3,0:T(8,128)} fusion(bf16[2,8,1024,2048]{3,2,0,1:T(8,128)(2,1)} %bitcast.332, pred[1024,2048]{1,0:T(8,128)(4,1)S(1)} %copy-done.11, bf16[2,4,2048,512]{3,2,0,1:T(8,128)(2,1)} %fusion.143), kind=kOutput, calls=%fused_computation.5 | convolution fusion | flops 17196646400 | bytes 60817408 | tf_op jit(solution)/shard_map/cfqp,cfpn->fqn/dot_general | solution.py:165
  440.0 6.5 %constant_dynamic-slice_fusion.1 = (f32[4,1,2,256,512]{4,3,2,1,0:T(8,128)}, f32[4,1,2,256,512]{4,3,2,1,0:T(8,128)S(1)}) fusion(f32[4,2,2,256,512]{4,3,2,1,0:T(8,128)} %bitcast.339, s32[]{:T(128)S(6)} %select_n.183, s32[]{:T(128)S(6)} %select_n.184), kind=kLoop, calls=%fused_computation.130 | loop fusion | bytes 16777224 | tf_op jit(solution)/shard_map/jit(dynamic_index_in_dim)/dynamic_slice | solution.py:13
  454.3 3.2 collective-permute-start.41
  457.5 3.0 fusion.31
  462.3 14.6 %collective-permute-done.34 = f16[4,256,512]{2,1,0:T(8,128)(2,1)} collective-permute-done((f16[4,256,512]{2,1,0:T(8,128)(2,1)S(1)}, f16[4,256,512]{2,1,0:T(8,128)(2,1)}, u32[]{:S(2)}, u32[]{:S(2)}) %collective-permute-start.34) | collective-permute-done | bytes 1048608 | tf_op jit(solution)/shard_map/ppermute | solution.py:96
  476.9 4.6 fusion.43
  483.1 14.8 %collective-permute-done.41 = f16[4,256,512]{2,1,0:T(8,128)(2,1)S(1)} collective-permute-done((f16[4,256,512]{2,1,0:T(8,128)(2,1)}, f16[4,256,512]{2,1,0:T(8,128)(2,1)S(1)}, u32[]{:S(2)}, u32[]{:S(2)}) %collective-permute-start.41) | collective-permute-done | bytes 1048608 | tf_op jit(solution)/shard_map/ppermute | solution.py:96
  497.9 3.1 fusion.33
  501.0 23.3 %collective-permute-start.42 = (f16[4,256,512]{2,1,0:T(8,128)(2,1)S(1)}, f16[4,256,512]{2,1,0:T(8,128)(2,1)S(1)}, u32[]{:S(2)}, u32[]{:S(2)}) collective-permute-start(f16[4,256,512]{2,1,0:T(8,128)(2,1)S(1)} %get-tuple-element.46), channel_id=1, source_target_pairs={{4,2},{5,3},{6,4},{7,5},{12,10},{13,11},{14,12},{15,13},{20,18},{2... | collective-permute-start | bytes 3145736 | tf_op jit(solution)/shard_map/ppermute | solution.py:96
  524.3 3.2 bitcast_add_fusion.1
  529.5 13.3 %collective-permute-done.36 = f32[4,2,256,512]{3,2,0,1:T(8,128)} collective-permute-done((f32[4,2,256,512]{3,2,0,1:T(8,128)}, f32[4,2,256,512]{3,2,0,1:T(8,128)}, u32[]{:S(2)}, u32[]{:S(2)}) %collective-permute-start.36) | collective-permute-done | bytes 4194336 | tf_op jit(solution)/shard_map/ppermute | solution.py:114
  542.8 3.2 bitcast_add_fusion
  550.4 3.0 fusion.29
  554.4 5.5 collective-permute-start.43
  559.9 12.1 %collective-permute-done.35 = f16[4,256,512]{2,1,0:T(8,128)(2,1)} collective-permute-done((f16[4,256,512]{2,1,0:T(8,128)(2,1)}, f16[4,256,512]{2,1,0:T(8,128)(2,1)}, u32[]{:S(2)}, u32[]{:S(2)}) %collective-permute-start.35) | collective-permute-done | bytes 1048608 | tf_op jit(solution)/shard_map/ppermute | solution.py:96
  572.0 14.2 %collective-permute-done.15 = f32[4,256,512]{2,1,0:T(8,128)} collective-permute-done((f32[4,256,512]{2,1,0:T(8,128)}, f32[4,256,512]{2,1,0:T(8,128)}, u32[]{:S(2)}, u32[]{:S(2)}) %collective-permute-start.15) | collective-permute-done | bytes 2097184 | tf_op jit(solution)/shard_map/ppermute | solution.py:114
  586.2 4.4 fusion.45
  592.8 3.9 fusion.35
  597.5 4.4 copy.59
  (170 shorter events, 93.9 us)
Async XLA Ops:
  4.8 66.3 %collective-permute-start.28 = (bf16[4,256,512]{2,1,0:T(8,128)(2,1)S(1)}, bf16[4,256,512]{2,1,0:T(8,128)(2,1)}, u32[]{:S(2)}, u32[]{:S(2)}) collective-permute-start(bf16[4,256,512]{2,1,0:T(8,128)(2,1)S(1)} %get-tuple-element.22), channel_id=1, source_target_pairs={{0,16},{8,24},{16,0},{24,8},{1,17},{9,25},{17,1},{25,9},{2,18},{10... | collective-permute-start | bytes 3145736 | tf_op jit(solution)/shard_map/ppermute | solution.py:62
  7.0 66.5 %collective-permute-start.10 = (bf16[4,256,512]{2,1,0:T(8,128)(2,1)S(1)}, bf16[4,256,512]{2,1,0:T(8,128)(2,1)}, u32[]{:S(2)}, u32[]{:S(2)}) collective-permute-start(bf16[4,256,512]{2,1,0:T(8,128)(2,1)S(1)} %get-tuple-element.24), channel_id=1, source_target_pairs={{0,8},{8,0},{16,24},{24,16},{1,9},{9,1},{17,25},{25,17},{2,10},{10... | collective-permute-start | bytes 3145736 | tf_op jit(solution)/shard_map/ppermute | solution.py:62
  8.5 80.2 %collective-permute-start.29 = (bf16[4,256,512]{2,1,0:T(8,128)(2,1)S(1)}, bf16[4,256,512]{2,1,0:T(8,128)(2,1)}, u32[]{:S(2)}, u32[]{:S(2)}) collective-permute-start(bf16[4,256,512]{2,1,0:T(8,128)(2,1)S(1)} %get-tuple-element.22), channel_id=1, source_target_pairs={{0,8},{8,0},{16,24},{24,16},{1,9},{9,1},{17,25},{25,17},{2,10},{10... | collective-permute-start | bytes 3145736 | tf_op jit(solution)/shard_map/ppermute | solution.py:62
  9.0 80.9 %collective-permute-start.11 = (bf16[4,256,512]{2,1,0:T(8,128)(2,1)S(1)}, bf16[4,256,512]{2,1,0:T(8,128)(2,1)}, u32[]{:S(2)}, u32[]{:S(2)}) collective-permute-start(bf16[4,256,512]{2,1,0:T(8,128)(2,1)S(1)} %get-tuple-element.24), channel_id=1, source_target_pairs={{0,16},{8,24},{16,0},{24,8},{1,17},{9,25},{17,1},{25,9},{2,18},{10... | collective-permute-start | bytes 3145736 | tf_op jit(solution)/shard_map/ppermute | solution.py:62
  9.6 85.1 %collective-permute-start = (bf16[4,256,512]{2,1,0:T(8,128)(2,1)S(1)}, bf16[4,256,512]{2,1,0:T(8,128)(2,1)}, u32[]{:S(2)}, u32[]{:S(2)}) collective-permute-start(bf16[4,256,512]{2,1,0:T(8,128)(2,1)S(1)} %get-tuple-element.24), channel_id=1, source_target_pairs={{0,1},{1,0},{2,3},{3,2},{4,5},{5,4},{6,7},{7,6},{8,9},{9,8},{10,11... | collective-permute-start | bytes 3145736 | tf_op jit(solution)/shard_map/ppermute | solution.py:17
  10.0 57.2 %dynamic-slice-start = ((s32[8192]{0:T(1024)}, s32[]{:T(128)}), s32[2048]{0:T(1024)S(1)}, s32[]{:S(2)}) async-start(s32[8192]{0:T(1024)} %param.6, s32[]{:T(128)} %select_n.157), calls=%async_computation | async-start | bytes 16896 | tf_op jit(solution)/shard_map/dynamic_slice | solution.py:133
  71.1 72.8 %copy-start.19 = (bf16[1,512,512]{2,1,0:T(8,128)(2,1)}, bf16[1,512,512]{2,1,0:T(8,128)(2,1)S(1)}, u32[]{:S(2)}) copy-start(bf16[1,512,512]{2,1,0:T(8,128)(2,1)S(1)} %get-tuple-element.62) | copy-start | bytes 1572868
  71.1 72.8 %copy-start.21 = (bf16[1,512,512]{2,1,0:T(8,128)(2,1)}, bf16[1,512,512]{2,1,0:T(8,128)(2,1)S(1)}, u32[]{:S(2)}) copy-start(bf16[1,512,512]{2,1,0:T(8,128)(2,1)S(1)} %get-tuple-element.63) | copy-start | bytes 1572868
  71.1 25.8 %collective-permute-start.2 = (bf16[4,256,512]{2,1,0:T(8,128)(2,1)S(1)}, bf16[4,256,512]{2,1,0:T(8,128)(2,1)S(1)}, u32[]{:S(2)}, u32[]{:S(2)}) collective-permute-start(bf16[4,256,512]{2,1,0:T(8,128)(2,1)S(1)} %get-tuple-element.24), channel_id=1, source_target_pairs={{2,0},{3,1},{4,2},{5,3},{6,4},{7,5},{10,8},{11,9},{12,10},{13,11},... | collective-permute-start | bytes 3145736 | tf_op jit(solution)/shard_map/ppermute | solution.py:47
  73.5 24.9 %collective-permute-start.16 = (bf16[4,256,512]{2,1,0:T(8,128)(2,1)S(1)}, bf16[4,256,512]{2,1,0:T(8,128)(2,1)S(1)}, u32[]{:S(2)}, u32[]{:S(2)}) collective-permute-start(bf16[4,256,512]{2,1,0:T(8,128)(2,1)S(1)} %get-tuple-element.22), channel_id=1, source_target_pairs={{0,1},{1,0},{2,3},{3,2},{4,5},{5,4},{6,7},{7,6},{8,9},{9,8},{10,11... | collective-permute-start | bytes 3145736 | tf_op jit(solution)/shard_map/ppermute | solution.py:17
  88.7 28.0 %collective-permute-start.1 = (bf16[4,256,512]{2,1,0:T(8,128)(2,1)S(1)}, bf16[4,256,512]{2,1,0:T(8,128)(2,1)}, u32[]{:S(2)}, u32[]{:S(2)}) collective-permute-start(bf16[4,256,512]{2,1,0:T(8,128)(2,1)S(1)} %get-tuple-element.24), channel_id=1, source_target_pairs={{0,2},{1,3},{2,4},{3,5},{4,6},{5,7},{8,10},{9,11},{10,12},{11,13},... | collective-permute-start | bytes 3145736 | tf_op jit(solution)/shard_map/ppermute | solution.py:46
  90.0 29.0 %collective-permute-start.18 = (bf16[4,256,512]{2,1,0:T(8,128)(2,1)S(1)}, bf16[4,256,512]{2,1,0:T(8,128)(2,1)S(1)}, u32[]{:S(2)}, u32[]{:S(2)}) collective-permute-start(bf16[4,256,512]{2,1,0:T(8,128)(2,1)S(1)} %get-tuple-element.22), channel_id=1, source_target_pairs={{2,0},{3,1},{4,2},{5,3},{6,4},{7,5},{10,8},{11,9},{12,10},{13,11},... | collective-permute-start | bytes 3145736 | tf_op jit(solution)/shard_map/ppermute | solution.py:47
  94.6 44.5 %collective-permute-start.17 = (bf16[4,256,512]{2,1,0:T(8,128)(2,1)S(1)}, bf16[4,256,512]{2,1,0:T(8,128)(2,1)}, u32[]{:S(2)}, u32[]{:S(2)}) collective-permute-start(bf16[4,256,512]{2,1,0:T(8,128)(2,1)S(1)} %get-tuple-element.22), channel_id=1, source_target_pairs={{0,2},{1,3},{2,4},{3,5},{4,6},{5,7},{8,10},{9,11},{10,12},{11,13},... | collective-permute-start | bytes 3145736 | tf_op jit(solution)/shard_map/ppermute | solution.py:46
  96.9 43.9 %collective-permute-start.12 = (bf16[4,256,512]{2,1,0:T(8,128)(2,1)}, bf16[4,256,512]{2,1,0:T(8,128)(2,1)S(1)}, u32[]{:S(2)}, u32[]{:S(2)}) collective-permute-start(bf16[4,256,512]{2,1,0:T(8,128)(2,1)} %collective-permute-done.10), channel_id=1, source_target_pairs={{0,16},{8,24},{16,0},{24,8},{1,17},{9,25},{17,1},{25,9},{2,18},{10... | collective-permute-start | bytes 3145736 | tf_op jit(solution)/shard_map/ppermute | solution.py:62
  98.4 43.7 %collective-permute-start.3 = (bf16[4,256,512]{2,1,0:T(8,128)(2,1)S(1)}, bf16[4,256,512]{2,1,0:T(8,128)(2,1)}, u32[]{:S(2)}, u32[]{:S(2)}) collective-permute-start(bf16[4,256,512]{2,1,0:T(8,128)(2,1)S(1)} %collective-permute-done.2), channel_id=1, source_target_pairs={{2,0},{3,1},{4,2},{5,3},{10,8},{11,9},{12,10},{13,11},{18,16},{19,... | collective-permute-start | bytes 3145736 | tf_op jit(solution)/shard_map/ppermute | solution.py:47
  116.7 62.2 %collective-permute-start.30 = (bf16[4,256,512]{2,1,0:T(8,128)(2,1)}, bf16[4,256,512]{2,1,0:T(8,128)(2,1)}, u32[]{:S(2)}, u32[]{:S(2)}) collective-permute-start(bf16[4,256,512]{2,1,0:T(8,128)(2,1)} %collective-permute-done.28), channel_id=1, source_target_pairs={{0,8},{8,0},{16,24},{24,16},{1,9},{9,1},{17,25},{25,17},{2,10},{10... | collective-permute-start | bytes 3145736 | tf_op jit(solution)/shard_map/ppermute | solution.py:62
  119.0 74.6 %collective-permute-start.6 = (bf16[4,256,512]{2,1,0:T(8,128)(2,1)}, bf16[4,256,512]{2,1,0:T(8,128)(2,1)}, u32[]{:S(2)}, u32[]{:S(2)}) collective-permute-start(bf16[4,256,512]{2,1,0:T(8,128)(2,1)} %collective-permute-done.1), channel_id=1, source_target_pairs={{2,4},{3,5},{4,6},{5,7},{10,12},{11,13},{12,14},{13,15},{18,20},{1... | collective-permute-start | bytes 3145736 | tf_op jit(solution)/shard_map/ppermute | solution.py:46
  139.1 11.4 %collective-permute-start.19 = (bf16[4,256,512]{2,1,0:T(8,128)(2,1)S(1)}, bf16[4,256,512]{2,1,0:T(8,128)(2,1)}, u32[]{:S(2)}, u32[]{:S(2)}) collective-permute-start(bf16[4,256,512]{2,1,0:T(8,128)(2,1)S(1)} %collective-permute-done.18), channel_id=1, source_target_pairs={{2,0},{3,1},{4,2},{5,3},{10,8},{11,9},{12,10},{13,11},{18,16},{19,... | collective-permute-start | bytes 3145736 | tf_op jit(solution)/shard_map/ppermute | solution.py:47
  140.8 54.1 %collective-permute-start.22 = (bf16[4,256,512]{2,1,0:T(8,128)(2,1)}, bf16[4,256,512]{2,1,0:T(8,128)(2,1)}, u32[]{:S(2)}, u32[]{:S(2)}) collective-permute-start(bf16[4,256,512]{2,1,0:T(8,128)(2,1)} %collective-permute-done.17), channel_id=1, source_target_pairs={{2,4},{3,5},{4,6},{5,7},{10,12},{11,13},{12,14},{13,15},{18,20},{1... | collective-permute-start | bytes 3145736 | tf_op jit(solution)/shard_map/ppermute | solution.py:46
  142.1 39.1 %collective-permute-start.4 = (bf16[4,256,512]{2,1,0:T(8,128)(2,1)}, bf16[4,256,512]{2,1,0:T(8,128)(2,1)}, u32[]{:S(2)}, u32[]{:S(2)}) collective-permute-start(bf16[4,256,512]{2,1,0:T(8,128)(2,1)} %collective-permute-done.3), channel_id=1, source_target_pairs={{2,0},{3,1},{10,8},{11,9},{18,16},{19,17},{26,24},{27,25}} | collective-permute-start | bytes 3145736 | tf_op jit(solution)/shard_map/ppermute | solution.py:47
  150.5 33.3 %collective-permute-start.20 = (bf16[4,256,512]{2,1,0:T(8,128)(2,1)}, bf16[4,256,512]{2,1,0:T(8,128)(2,1)}, u32[]{:S(2)}, u32[]{:S(2)}) collective-permute-start(bf16[4,256,512]{2,1,0:T(8,128)(2,1)} %collective-permute-done.19), channel_id=1, source_target_pairs={{2,0},{3,1},{10,8},{11,9},{18,16},{19,17},{26,24},{27,25}} | collective-permute-start | bytes 3145736 | tf_op jit(solution)/shard_map/ppermute | solution.py:47
  183.9 12.5 %collective-permute-start.5 = (bf16[4,256,512]{2,1,0:T(8,128)(2,1)S(1)}, bf16[4,256,512]{2,1,0:T(8,128)(2,1)S(1)}, u32[]{:S(2)}, u32[]{:S(2)}) collective-permute-start(bf16[4,256,512]{2,1,0:T(8,128)(2,1)S(1)} %get-tuple-element.30), channel_id=1, source_target_pairs={{0,1},{1,0},{2,3},{3,2},{4,5},{5,4},{6,7},{7,6},{8,9},{9,8},{10,11... | collective-permute-start | bytes 3145736 | tf_op jit(solution)/shard_map/ppermute | solution.py:17
  186.4 13.6 %collective-permute-start.21 = (bf16[4,256,512]{2,1,0:T(8,128)(2,1)S(1)}, bf16[4,256,512]{2,1,0:T(8,128)(2,1)S(1)}, u32[]{:S(2)}, u32[]{:S(2)}) collective-permute-start(bf16[4,256,512]{2,1,0:T(8,128)(2,1)S(1)} %get-tuple-element.36), channel_id=1, source_target_pairs={{0,1},{1,0},{2,3},{3,2},{4,5},{5,4},{6,7},{7,6},{8,9},{9,8},{10,11... | collective-permute-start | bytes 3145736 | tf_op jit(solution)/shard_map/ppermute | solution.py:17
  193.6 39.3 %collective-permute-start.8 = (bf16[4,256,512]{2,1,0:T(8,128)(2,1)}, bf16[4,256,512]{2,1,0:T(8,128)(2,1)S(1)}, u32[]{:S(2)}, u32[]{:S(2)}) collective-permute-start(bf16[4,256,512]{2,1,0:T(8,128)(2,1)} %collective-permute-done.6), channel_id=1, source_target_pairs={{4,6},{5,7},{12,14},{13,15},{20,22},{21,23},{28,30},{29,31}} | collective-permute-start | bytes 3145736 | tf_op jit(solution)/shard_map/ppermute | solution.py:46
  194.9 59.8 %collective-permute-start.24 = (bf16[4,256,512]{2,1,0:T(8,128)(2,1)}, bf16[4,256,512]{2,1,0:T(8,128)(2,1)S(1)}, u32[]{:S(2)}, u32[]{:S(2)}) collective-permute-start(bf16[4,256,512]{2,1,0:T(8,128)(2,1)} %collective-permute-done.22), channel_id=1, source_target_pairs={{4,6},{5,7},{12,14},{13,15},{20,22},{21,23},{28,30},{29,31}} | collective-permute-start | bytes 3145736 | tf_op jit(solution)/shard_map/ppermute | solution.py:46
  200.0 18.0 %collective-permute-start.7 = (bf16[4,256,512]{2,1,0:T(8,128)(2,1)S(1)}, bf16[4,256,512]{2,1,0:T(8,128)(2,1)S(1)}, u32[]{:S(2)}, u32[]{:S(2)}) collective-permute-start(bf16[4,256,512]{2,1,0:T(8,128)(2,1)S(1)} %get-tuple-element.28), channel_id=1, source_target_pairs={{0,1},{1,0},{2,3},{3,2},{4,5},{5,4},{6,7},{7,6},{8,9},{9,8},{10,11... | collective-permute-start | bytes 3145736 | tf_op jit(solution)/shard_map/ppermute | solution.py:17
  203.6 30.9 %collective-permute-start.23 = (bf16[4,256,512]{2,1,0:T(8,128)(2,1)S(1)}, bf16[4,256,512]{2,1,0:T(8,128)(2,1)S(1)}, u32[]{:S(2)}, u32[]{:S(2)}) collective-permute-start(bf16[4,256,512]{2,1,0:T(8,128)(2,1)S(1)} %get-tuple-element.34), channel_id=1, source_target_pairs={{0,1},{1,0},{2,3},{3,2},{4,5},{5,4},{6,7},{7,6},{8,9},{9,8},{10,11... | collective-permute-start | bytes 3145736 | tf_op jit(solution)/shard_map/ppermute | solution.py:17
  218.0 83.6 %collective-permute-start.13 = (f32[4,4,256,512]{3,2,0,1:T(8,128)}, f32[4,4,256,512]{3,2,0,1:T(8,128)}, u32[]{:S(2)}, u32[]{:S(2)}) collective-permute-start(f32[4,4,256,512]{3,2,0,1:T(8,128)} %bitcast.334), channel_id=1, source_target_pairs={{0,1},{1,0},{2,3},{3,2},{4,5},{5,4},{6,7},{7,6},{8,9},{9,8},{10,11... | collective-permute-start | bytes 25165832 | tf_op jit(solution)/shard_map/ppermute | solution.py:17
  234.5 62.6 %collective-permute-start.9 = (bf16[4,256,512]{2,1,0:T(8,128)(2,1)}, bf16[4,256,512]{2,1,0:T(8,128)(2,1)}, u32[]{:S(2)}, u32[]{:S(2)}) collective-permute-start(bf16[4,256,512]{2,1,0:T(8,128)(2,1)} %get-tuple-element.26), channel_id=1, source_target_pairs={{0,1},{1,0},{2,3},{3,2},{4,5},{5,4},{6,7},{7,6},{8,9},{9,8},{10,11... | collective-permute-start | bytes 3145736 | tf_op jit(solution)/shard_map/ppermute | solution.py:17
  256.0 43.3 %collective-permute-start.25 = (bf16[4,256,512]{2,1,0:T(8,128)(2,1)S(1)}, bf16[4,256,512]{2,1,0:T(8,128)(2,1)}, u32[]{:S(2)}, u32[]{:S(2)}) collective-permute-start(bf16[4,256,512]{2,1,0:T(8,128)(2,1)S(1)} %get-tuple-element.32), channel_id=1, source_target_pairs={{0,1},{1,0},{2,3},{3,2},{4,5},{5,4},{6,7},{7,6},{8,9},{9,8},{10,11... | collective-permute-start | bytes 3145736 | tf_op jit(solution)/shard_map/ppermute | solution.py:17
  296.5 78.6 %collective-permute-start.31 = (f32[4,4,256,512]{3,2,0,1:T(8,128)}, f32[4,4,256,512]{3,2,0,1:T(8,128)}, u32[]{:S(2)}, u32[]{:S(2)}) collective-permute-start(f32[4,4,256,512]{3,2,0,1:T(8,128)} %bitcast.333), channel_id=1, source_target_pairs={{0,1},{1,0},{2,3},{3,2},{4,5},{5,4},{6,7},{7,6},{8,9},{9,8},{10,11... | collective-permute-start | bytes 25165832 | tf_op jit(solution)/shard_map/ppermute | solution.py:17
  317.3 73.5 %collective-permute-start.26 = (f16[4,256,512]{2,1,0:T(8,128)(2,1)}, f16[4,256,512]{2,1,0:T(8,128)(2,1)S(1)}, u32[]{:S(2)}, u32[]{:S(2)}) collective-permute-start(f16[4,256,512]{2,1,0:T(8,128)(2,1)} %get-tuple-element.14), channel_id=1, source_target_pairs={{0,2},{1,3},{8,10},{9,11},{16,18},{17,19},{24,26},{25,27}} | collective-permute-start | bytes 3145736 | tf_op jit(solution)/shard_map/ppermute | solution.py:95
  318.0 73.8 %collective-permute-start.27 = (f16[4,256,512]{2,1,0:T(8,128)(2,1)}, f16[4,256,512]{2,1,0:T(8,128)(2,1)}, u32[]{:S(2)}, u32[]{:S(2)}) collective-permute-start(f16[4,256,512]{2,1,0:T(8,128)(2,1)} %get-tuple-element.15), channel_id=1, source_target_pairs={{6,4},{7,5},{14,12},{15,13},{22,20},{23,21},{30,28},{31,29}} | collective-permute-start | bytes 3145736 | tf_op jit(solution)/shard_map/ppermute | solution.py:96
  373.6 150.7 %collective-permute-start.14 = (f32[4,2,256,512]{3,2,0,1:T(8,128)}, f32[4,2,256,512]{3,2,0,1:T(8,128)}, u32[]{:S(2)}, u32[]{:S(2)}) collective-permute-start(f32[4,2,256,512]{3,2,0,1:T(8,128)} %bitcast.336), channel_id=1, source_target_pairs={{0,8},{8,0},{16,24},{24,16},{1,9},{9,1},{17,25},{25,17},{2,10},{10... | collective-permute-start | bytes 12582920 | tf_op jit(solution)/shard_map/ppermute | solution.py:114
  449.0 93.8 %collective-permute-start.36 = (f32[4,2,256,512]{3,2,0,1:T(8,128)}, f32[4,2,256,512]{3,2,0,1:T(8,128)}, u32[]{:S(2)}, u32[]{:S(2)}) collective-permute-start(f32[4,2,256,512]{3,2,0,1:T(8,128)} %bitcast.335), channel_id=1, source_target_pairs={{0,16},{8,24},{16,0},{24,8},{1,17},{9,25},{17,1},{25,9},{2,18},{10... | collective-permute-start | bytes 12582920 | tf_op jit(solution)/shard_map/ppermute | solution.py:114
  450.5 3.8 collective-permute-start.38
  451.2 9.3 %collective-permute-start.32 = (f16[4,256,512]{2,1,0:T(8,128)(2,1)S(1)}, f16[4,256,512]{2,1,0:T(8,128)(2,1)S(1)}, u32[]{:S(2)}, u32[]{:S(2)}) collective-permute-start(f16[4,256,512]{2,1,0:T(8,128)(2,1)S(1)} %copy-done.14), channel_id=1, source_target_pairs={{0,2},{1,3},{2,4},{3,5},{8,10},{9,11},{10,12},{11,13},{16,18},{17,... | collective-permute-start | bytes 3145736 | tf_op jit(solution)/shard_map/ppermute | solution.py:95
  452.0 24.9 %collective-permute-start.34 = (f16[4,256,512]{2,1,0:T(8,128)(2,1)S(1)}, f16[4,256,512]{2,1,0:T(8,128)(2,1)}, u32[]{:S(2)}, u32[]{:S(2)}) collective-permute-start(f16[4,256,512]{2,1,0:T(8,128)(2,1)S(1)} %get-tuple-element.17), channel_id=1, source_target_pairs={{4,2},{5,3},{6,4},{7,5},{12,10},{13,11},{14,12},{15,13},{20,18},{2... | collective-permute-start | bytes 3145736 | tf_op jit(solution)/shard_map/ppermute | solution.py:96
  454.3 43.6 %collective-permute-start.41 = (f16[4,256,512]{2,1,0:T(8,128)(2,1)}, f16[4,256,512]{2,1,0:T(8,128)(2,1)S(1)}, u32[]{:S(2)}, u32[]{:S(2)}) collective-permute-start(f16[4,256,512]{2,1,0:T(8,128)(2,1)} %get-tuple-element.20), channel_id=1, source_target_pairs={{6,4},{7,5},{14,12},{15,13},{22,20},{23,21},{30,28},{31,29}} | collective-permute-start | bytes 3145736 | tf_op jit(solution)/shard_map/ppermute | solution.py:96
  461.5 36.3 %collective-permute-start.39 = (f16[4,256,512]{2,1,0:T(8,128)(2,1)}, f16[4,256,512]{2,1,0:T(8,128)(2,1)S(1)}, u32[]{:S(2)}, u32[]{:S(2)}) collective-permute-start(f16[4,256,512]{2,1,0:T(8,128)(2,1)} %fusion.31), channel_id=1, source_target_pairs={{0,2},{1,3},{2,4},{3,5},{8,10},{9,11},{10,12},{11,13},{16,18},{17,... | collective-permute-start | bytes 3145736 | tf_op jit(solution)/shard_map/ppermute | solution.py:95
  481.5 42.8 %copy-start.5 = (f32[4,2,1,256,512]{4,3,2,1,0:T(8,128)S(1)}, f32[4,2,1,256,512]{4,3,2,1,0:T(8,128)}, u32[]{:S(2)}) copy-start(f32[4,2,1,256,512]{4,3,2,1,0:T(8,128)} %get-tuple-element.43) | copy-start | bytes 12582916
  481.5 71.9 %collective-permute-start.33 = (f16[4,256,512]{2,1,0:T(8,128)(2,1)S(1)}, f16[4,256,512]{2,1,0:T(8,128)(2,1)S(1)}, u32[]{:S(2)}, u32[]{:S(2)}) collective-permute-start(f16[4,256,512]{2,1,0:T(8,128)(2,1)S(1)} %get-tuple-element.41), channel_id=1, source_target_pairs={{0,2},{1,3},{2,4},{3,5},{4,6},{5,7},{8,10},{9,11},{10,12},{11,13},... | collective-permute-start | bytes 3145736 | tf_op jit(solution)/shard_map/ppermute | solution.py:95
  501.0 48.1 %collective-permute-start.42 = (f16[4,256,512]{2,1,0:T(8,128)(2,1)S(1)}, f16[4,256,512]{2,1,0:T(8,128)(2,1)S(1)}, u32[]{:S(2)}, u32[]{:S(2)}) collective-permute-start(f16[4,256,512]{2,1,0:T(8,128)(2,1)S(1)} %get-tuple-element.46), channel_id=1, source_target_pairs={{4,2},{5,3},{6,4},{7,5},{12,10},{13,11},{14,12},{15,13},{20,18},{2... | collective-permute-start | bytes 3145736 | tf_op jit(solution)/shard_map/ppermute | solution.py:96
  529.0 57.2 %collective-permute-start.15 = (f32[4,256,512]{2,1,0:T(8,128)}, f32[4,256,512]{2,1,0:T(8,128)}, u32[]{:S(2)}, u32[]{:S(2)}) collective-permute-start(f32[4,256,512]{2,1,0:T(8,128)} %dynamic-slice_bitcast_fusion.1), channel_id=1, source_target_pairs={{0,16},{8,24},{16,0},{24,8},{1,17},{9,25},{17,1},{25,9},{2,18},{10... | collective-permute-start | bytes 6291464 | tf_op jit(solution)/shard_map/ppermute | solution.py:114
  546.2 44.7 %collective-permute-start.37 = (f32[4,256,512]{2,1,0:T(8,128)S(1)}, f32[4,256,512]{2,1,0:T(8,128)}, u32[]{:S(2)}, u32[]{:S(2)}) collective-permute-start(f32[4,256,512]{2,1,0:T(8,128)S(1)} %dynamic-slice_bitcast_fusion), channel_id=1, source_target_pairs={{0,8},{8,0},{16,24},{24,16},{1,9},{9,1},{17,25},{25,17},{2,10},{10... | collective-permute-start | bytes 6291464 | tf_op jit(solution)/shard_map/ppermute | solution.py:114
  546.8 25.2 %collective-permute-start.35 = (f16[4,256,512]{2,1,0:T(8,128)(2,1)}, f16[4,256,512]{2,1,0:T(8,128)(2,1)}, u32[]{:S(2)}, u32[]{:S(2)}) collective-permute-start(f16[4,256,512]{2,1,0:T(8,128)(2,1)} %get-tuple-element.42), channel_id=1, source_target_pairs={{2,0},{3,1},{4,2},{5,3},{6,4},{7,5},{10,8},{11,9},{12,10},{13,11},... | collective-permute-start | bytes 3145736 | tf_op jit(solution)/shard_map/ppermute | solution.py:96
  549.1 41.7 %collective-permute-start.40 = (f16[4,256,512]{2,1,0:T(8,128)(2,1)S(1)}, f16[4,256,512]{2,1,0:T(8,128)(2,1)}, u32[]{:S(2)}, u32[]{:S(2)}) collective-permute-start(f16[4,256,512]{2,1,0:T(8,128)(2,1)S(1)} %get-tuple-element.45), channel_id=1, source_target_pairs={{0,2},{1,3},{2,4},{3,5},{4,6},{5,7},{8,10},{9,11},{10,12},{11,13},... | collective-permute-start | bytes 3145736 | tf_op jit(solution)/shard_map/ppermute | solution.py:95
  554.4 36.4 %collective-permute-start.43 = (f16[4,256,512]{2,1,0:T(8,128)(2,1)}, f16[4,256,512]{2,1,0:T(8,128)(2,1)}, u32[]{:S(2)}, u32[]{:S(2)}) collective-permute-start(f16[4,256,512]{2,1,0:T(8,128)(2,1)} %fusion.29), channel_id=1, source_target_pairs={{2,0},{3,1},{4,2},{5,3},{6,4},{7,5},{10,8},{11,9},{12,10},{13,11},... | collective-permute-start | bytes 3145736 | tf_op jit(solution)/shard_map/ppermute | solution.py:96
  (21 other events, 173.4 us)

commit v2 on v1

--- a/solution.py
+++ b/solution.py
@@ -162,8 +162,12 @@
             for i, line_sum in enumerate(ready):
                 line_sum.out = sent[2 * i : 2 * i + 2]
                 line_sum.send()
+            spec = both(spec, -1)
+            if len(ready) > 1:
+                early = ready[0]
+                spec, early.right, early.left = after(spec, early.right, early.left)
             col_part = jnp.einsum(
-                "cfqp,cfpn->fqn", masked[k], both(spec, -1), preferred_element_type=jnp.float32
+                "cfqp,cfpn->fqn", masked[k], spec, preferred_element_type=jnp.float32
             )
             outs.append(reduce_cube(col_part, row, n_row, orders[k]))
         totals = [x + line_sum.total() for x, line_sum in zip(outs, sums)]

time: 612 us -> 630 us (1.029)
  waiting for transfers between devices: 132 us -> 141 us
  starting transfers between devices: 79.6 us -> 87.6 us
    ppermute x6, waiting for transfers between devices: 41.5 us -> 17.5 us  [send(): lax.ppermute(self.out[1], 'col', line_perm(range(line - step, line), -1,...]
    ppermute x6, waiting for transfers between devices: 0.02 us -> 18.2 us  [send(): right = lax.ppermute(self.out[0], 'col', line_perm(range(step), 1, n_col))]
    ppermute x4, waiting for transfers between devices: 27.6 us -> 35.7 us  [reduce_cube(): lax.ppermute(pick(part, 1 - high, axis), 'row', perm)]
    ppermute x6, waiting for transfers between devices: 61.4 us -> 69.1 us  [gather_line(): lax.ppermute(to_right[-1], 'col', line_perm(range(step, line), 1, n_col))]
    unnamed x51 -> x55, local copies, waits for them, and re-layouts: 15.7 us -> 12.8 us
  transfers between devices with their start and end apart: 44 -> 44, of which waited for: 12 -> 10; matrix products, arithmetic and copies ran while one was open for 62% -> 60% of each run, Pallas kernels for 0% -> 0%
where the time goes in v2:
time: 630 us; the launch traced here: 618 us
  matrix products  153 us (24%)
  local copies, waits for them, and re-layouts  149 us (24%)
  waiting for transfers between devices  141 us (22%)
  starting transfers between devices  87.6 us (14%)
  other arithmetic  86.4 us (14%)
    ppermute x6, waiting for transfers between devices, gather_line(): lax.ppermute(to_right[-1], 'col', line_perm(range(step, line), 1, n_col))  69.1 us
    reshape x1, local copies, waits for them, and re-layouts, body(): grads = pair_grad.reshape(blocks * width_b, 2, bins, block_p)  57.2 us
    dot_general x2, matrix products, body(): jnp.einsum('cfqp,cfpn->fqn', masked[k], spec, preferred_element_type=jnp....  54.6 us
    dot_general x2, matrix products, body(): jnp.einsum('cfqp,cfqn->fpn', masked[k], both(col_specs[k], 1), preferred_...  53.1 us
    dot_general x4, matrix products, both(): jnp.einsum('fin,cnm->cfim', spec, jnp.stack([same, turn]), preferred_elem...  45.7 us
    ppermute x6, starting transfers between devices, send(): lax.ppermute(self.out[1], 'col', line_perm(range(line - step, line), -1,...  43.5 us
    dynamic_slice x7, local copies, waits for them, and re-layouts, pick(): return lax.dynamic_index_in_dim(x, index, axis, keepdims=False)  37.2 us
    ppermute x4, waiting for transfers between devices, reduce_cube(): lax.ppermute(pick(part, 1 - high, axis), 'row', perm)  35.7 us
  transfers between devices with their start and end apart: 44, of which 10 were waited for; matrix products, arithmetic and copies ran while one was open for 60% of the time, Pallas kernels for 0%

profile of v2, /device:TPU:24, one launch (start us, length us, event | category | flops | bytes accessed | tf_op | source)
XLA Modules:
  0.0 618.0 jit_solution(940081486441828880)
XLA Ops:
  11.5 57.2 %copy.98 = bf16[1024,2,8,2048]{3,0,1,2:T(8,128)(2,1)} copy(bf16[1024,2,8,2048]{3,2,1,0:T(8,128)(2,1)} %bitcast.5) | data formatting | bytes 134217728 | tf_op jit(solution)/shard_map/reshape | solution.py:141
  69.3 2.8 bitcast_and_fusion
  74.2 4.3 broadcast.55.clone
  79.5 4.3 broadcast.55.clone.1
  84.9 2.9 bitcast_dynamic-update-slice_fusion.16
  92.6 5.2 collective-permute-start.2
  107.0 11.1 %collective-permute-done.17 = bf16[4,256,512]{2,1,0:T(8,128)(2,1)} collective-permute-done((bf16[4,256,512]{2,1,0:T(8,128)(2,1)S(1)}, bf16[4,256,512]{2,1,0:T(8,128)(2,1)}, u32[]{:S(2)}, u32[]{:S(2)}) %collective-permute-start.17) | collective-permute-done | bytes 1048608 | tf_op jit(solution)/shard_map/ppermute | solution.py:46
  119.6 18.6 %collective-permute-done.1 = bf16[4,256,512]{2,1,0:T(8,128)(2,1)} collective-permute-done((bf16[4,256,512]{2,1,0:T(8,128)(2,1)S(1)}, bf16[4,256,512]{2,1,0:T(8,128)(2,1)}, u32[]{:S(2)}, u32[]{:S(2)}) %collective-permute-start.1) | collective-permute-done | bytes 1048608 | tf_op jit(solution)/shard_map/ppermute | solution.py:46
  144.2 6.8 %fusion.122 = bf16[2,4,1024,512]{3,2,0,1:T(8,128)(2,1)} fusion(bf16[4,1024,512,1]{2,1,3,0:T(8,128)(2,1)S(1)} %bitcast.323, bf16[1,512,512]{1,2,0:T(8,128)(2,1)S(1)} %get-tuple-element.68, bf16[1,512,512]{1,2,0:T(8,128)(2,1)S(1)} %get-tuple-element.69), kind=kOutput, calls=%fused_computation.24.clone.2 | convolution fusion | flops 4297064448 | bytes 13631488 | tf_op jit(solution)/shard_map/fin,cnm->cfim/dot_general | solution.py:39
  152.9 26.6 %fusion.1 = f32[4,2048,512,1]{2,1,3,0:T(8,128)} fusion(bf16[2,8,1024,2048]{3,2,0,1:T(8,128)(2,1)} %bitcast.314, pred[1024,2048]{1,0:T(8,128)(4,1)S(1)} %copy-done.11, bf16[2,4,1024,512]{3,2,0,1:T(8,128)(2,1)} %fusion.122), kind=kOutput, calls=%fused_computation.4 | convolution fusion | flops 17196646400 | bytes 60817408 | tf_op jit(solution)/shard_map/cfqp,cfqn->fpn/dot_general | solution.py:149
  182.0 2.5 bitcast_dynamic-update-slice_fusion.12
  185.0 9.5 %constant_dynamic-slice_fusion.7 = (f32[4,4,1,256,512]{4,3,2,1,0:T(8,128)}, f32[4,4,1,256,512]{4,3,2,1,0:T(8,128)S(1)}) fusion(f32[4,4,2,256,512]{4,3,2,1,0:T(8,128)} %bitcast.319, s32[]{:T(128)S(6)} %select_n.179, s32[]{:T(128)S(6)} %select_n.180), kind=kLoop, calls=%fused_computation.139 | loop fusion | bytes 33554440 | tf_op jit(solution)/shard_map/jit(dynamic_index_in_dim)/dynamic_slice | solution.py:13
  194.5 4.4 copy.100
  211.1 6.8 %fusion.126 = bf16[2,4,1024,512]{3,2,0,1:T(8,128)(2,1)} fusion(bf16[4,1024,512,1]{2,1,3,0:T(8,128)(2,1)S(1)} %bitcast.324, bf16[1,512,512]{1,2,0:T(8,128)(2,1)S(1)} %copy-done.20, bf16[1,512,512]{1,2,0:T(8,128)(2,1)S(1)} %copy-done.24), kind=kOutput, calls=%fused_computation.23.clone.2 | convolution fusion | flops 4297064448 | bytes 13631488 | tf_op jit(solution)/shard_map/fin,cnm->cfim/dot_general | solution.py:39
  219.0 19.9 %collective-permute-done.24 = bf16[4,256,512]{2,1,0:T(8,128)(2,1)S(1)} collective-permute-done((bf16[4,256,512]{2,1,0:T(8,128)(2,1)}, bf16[4,256,512]{2,1,0:T(8,128)(2,1)S(1)}, u32[]{:S(2)}, u32[]{:S(2)}) %collective-permute-start.24) | collective-permute-done | bytes 1048608 | tf_op jit(solution)/shard_map/ppermute | solution.py:46
  241.6 19.6 %collective-permute-done.8 = bf16[4,256,512]{2,1,0:T(8,128)(2,1)S(1)} collective-permute-done((bf16[4,256,512]{2,1,0:T(8,128)(2,1)}, bf16[4,256,512]{2,1,0:T(8,128)(2,1)S(1)}, u32[]{:S(2)}, u32[]{:S(2)}) %collective-permute-start.8) | collective-permute-done | bytes 1048608 | tf_op jit(solution)/shard_map/ppermute | solution.py:46
  262.5 26.6 %fusion.3 = f32[4,2048,512,1]{2,1,3,0:T(8,128)} fusion(bf16[2,8,1024,2048]{3,2,0,1:T(8,128)(2,1)} %bitcast.314, pred[1024,2048]{1,0:T(8,128)(4,1)S(1)} %copy-done.11, bf16[2,4,1024,512]{3,2,0,1:T(8,128)(2,1)} %fusion.126), kind=kOutput, calls=%fused_computation.6 | convolution fusion | flops 17196646400 | bytes 60817408 | tf_op jit(solution)/shard_map/cfqp,cfqn->fpn/dot_general | solution.py:149
  289.1 9.5 %constant_dynamic-slice_fusion.3 = (f32[4,4,1,256,512]{4,3,2,1,0:T(8,128)}, f32[4,4,1,256,512]{4,3,2,1,0:T(8,128)S(1)}) fusion(f32[4,4,2,256,512]{4,3,2,1,0:T(8,128)} %bitcast.320, s32[]{:T(128)S(6)} %select_n.179, s32[]{:T(128)S(6)} %select_n.180), kind=kLoop, calls=%fused_computation.135 | loop fusion | bytes 33554440 | tf_op jit(solution)/shard_map/jit(dynamic_index_in_dim)/dynamic_slice | solution.py:13
  298.6 4.3 copy.99
  307.9 11.5 %fusion.11 = f32[4,4,256,512]{3,2,0,1:T(8,128)} fusion(f32[4,4,256,512]{3,2,0,1:T(8,128)} %collective-permute-done.13, f32[4,4,1,256,512]{4,3,2,1,0:T(8,128)} %get-tuple-element.45), kind=kLoop, calls=%fused_computation.19 | loop fusion | flops 2097152 | bytes 25165824 | tf_op jit(solution)/shard_map/add | solution.py:85
  319.4 4.2 fusion.43
  326.9 16.1 %fusion.118 = bf16[2,4,2048,512]{3,2,0,1:T(8,128)(2,1)} fusion(bf16[4,2048,512]{2,1,0:T(8,128)(2,1)} %bitcast.28, bf16[1,512,512]{1,2,0:T(8,128)(2,1)S(1)} %copy-done.21, bf16[1,512,512]{1,2,0:T(8,128)(2,1)S(1)} %copy-done.17), kind=kOutput, calls=%fused_computation.8.clone.2 | convolution fusion | flops 8592031744 | bytes 26214400 | tf_op jit(solution)/shard_map/fin,cnm->cfim/dot_general | solution.py:39
  343.1 28.9 %fusion = f32[4,1024,512,1]{2,1,3,0:T(8,128)} fusion(bf16[2,8,1024,2048]{3,2,0,1:T(8,128)(2,1)} %bitcast.314, pred[1024,2048]{1,0:T(8,128)(4,1)S(1)} %copy-done.11, bf16[2,4,2048,512]{3,2,0,1:T(8,128)(2,1)} %fusion.118), kind=kOutput, calls=%fused_computation.3 | convolution fusion | flops 17196646400 | bytes 60817408 | tf_op jit(solution)/shard_map/cfqp,cfpn->fqn/dot_general | solution.py:169
  372.0 6.6 %constant_dynamic-slice_fusion.5 = (f32[4,2,1,256,512]{4,3,2,1,0:T(8,128)}, f32[4,2,1,256,512]{4,3,2,1,0:T(8,128)S(1)}) fusion(f32[4,2,2,256,512]{4,3,2,1,0:T(8,128)} %bitcast.322, s32[]{:T(128)S(6)} %select_n.181, s32[]{:T(128)S(6)} %select_n.182), kind=kLoop, calls=%fused_computation.137 | loop fusion | bytes 16777224 | tf_op jit(solution)/shard_map/jit(dynamic_index_in_dim)/dynamic_slice | solution.py:13
  382.7 11.6 %fusion.10 = f32[4,4,256,512]{3,2,0,1:T(8,128)} fusion(f32[4,4,256,512]{3,2,0,1:T(8,128)} %collective-permute-done.31, f32[4,4,1,256,512]{4,3,2,1,0:T(8,128)} %get-tuple-element.43), kind=kLoop, calls=%fused_computation.16 | loop fusion | flops 2097152 | bytes 25165824 | tf_op jit(solution)/shard_map/add | solution.py:85
  394.2 4.2 fusion.45
  398.4 4.4 fusion.34
  405.8 15.9 %convolution_bitcast_fusion = bf16[2,4,2048,512]{2,3,1,0:T(8,128)(2,1)} fusion(bf16[4,2048,512]{2,1,0:T(8,128)(2,1)} %bitcast.74, bf16[1,512,512]{1,2,0:T(8,128)(2,1)S(1)} %copy-done.22, bf16[1,512,512]{1,2,0:T(8,128)(2,1)S(1)} %copy-done.18), kind=kOutput, calls=%fused_computation.13 | convolution fusion | flops 8592031744 | bytes 26214400 | tf_op jit(solution)/shard_map/fin,cnm->cfim/dot_general | solution.py:39
  423.3 5.1 collective-permute-done.33
  430.0 25.7 %fusion.2 = f32[4,1024,512,1]{2,1,3,0:T(8,128)} fusion(bf16[2,8,1024,2048]{3,2,0,1:T(8,128)(2,1)} %bitcast.314, pred[1024,2048]{1,0:T(8,128)(4,1)} %bitcast_and_fusion, bf16[2,4,2048,512]{2,3,1,0:T(8,128)(2,1)} %convolution_bitcast_fusion), kind=kOutput, calls=%fused_computation.5 | convolution fusion | flops 17196646400 | bytes 60817408 | tf_op jit(solution)/shard_map/cfqp,cfpn->fqn/dot_general | solution.py:169
  455.7 6.5 %constant_dynamic-slice_fusion.1 = (f32[4,1,2,256,512]{4,3,2,1,0:T(8,128)}, f32[4,1,2,256,512]{4,3,2,1,0:T(8,128)S(1)}) fusion(f32[4,2,2,256,512]{4,3,2,1,0:T(8,128)} %bitcast.321, s32[]{:T(128)S(6)} %select_n.183, s32[]{:T(128)S(6)} %select_n.184), kind=kLoop, calls=%fused_computation.133 | loop fusion | bytes 16777224 | tf_op jit(solution)/shard_map/jit(dynamic_index_in_dim)/dynamic_slice | solution.py:13
  466.9 4.3 collective-permute-start.41
  471.3 3.1 fusion.26
  475.9 5.0 fusion.38
  482.7 12.4 %collective-permute-done.41 = f16[4,256,512]{2,1,0:T(8,128)(2,1)S(1)} collective-permute-done((f16[4,256,512]{2,1,0:T(8,128)(2,1)}, f16[4,256,512]{2,1,0:T(8,128)(2,1)S(1)}, u32[]{:S(2)}, u32[]{:S(2)}) %collective-permute-start.41) | collective-permute-done | bytes 1048608 | tf_op jit(solution)/shard_map/ppermute | solution.py:96
  496.1 3.7 fusion.28
  499.7 27.9 %collective-permute-start.42 = (f16[4,256,512]{2,1,0:T(8,128)(2,1)S(1)}, f16[4,256,512]{2,1,0:T(8,128)(2,1)S(1)}, u32[]{:S(2)}, u32[]{:S(2)}) collective-permute-start(f16[4,256,512]{2,1,0:T(8,128)(2,1)S(1)} %get-tuple-element.52), channel_id=1, source_target_pairs={{4,2},{5,3},{6,4},{7,5},{12,10},{13,11},{14,12},{15,13},{20,18},{2... | collective-permute-start | bytes 3145736 | tf_op jit(solution)/shard_map/ppermute | solution.py:96
  527.6 3.2 bitcast_add_fusion.1
  532.9 25.6 %collective-permute-done.36 = f32[4,2,256,512]{3,2,0,1:T(8,128)} collective-permute-done((f32[4,2,256,512]{3,2,0,1:T(8,128)}, f32[4,2,256,512]{3,2,0,1:T(8,128)}, u32[]{:S(2)}, u32[]{:S(2)}) %collective-permute-start.36) | collective-permute-done | bytes 4194336 | tf_op jit(solution)/shard_map/ppermute | solution.py:114
  558.5 3.2 bitcast_add_fusion
  565.1 3.0 fusion.24
  569.1 6.5 %collective-permute-start.43 = (f16[4,256,512]{2,1,0:T(8,128)(2,1)}, f16[4,256,512]{2,1,0:T(8,128)(2,1)}, u32[]{:S(2)}, u32[]{:S(2)}) collective-permute-start(f16[4,256,512]{2,1,0:T(8,128)(2,1)} %fusion.24), channel_id=1, source_target_pairs={{2,0},{3,1},{4,2},{5,3},{6,4},{7,5},{10,8},{11,9},{12,10},{13,11},... | collective-permute-start | bytes 3145736 | tf_op jit(solution)/shard_map/ppermute | solution.py:96
  575.6 15.5 %collective-permute-done.34 = f16[4,256,512]{2,1,0:T(8,128)(2,1)} collective-permute-done((f16[4,256,512]{2,1,0:T(8,128)(2,1)}, f16[4,256,512]{2,1,0:T(8,128)(2,1)}, u32[]{:S(2)}, u32[]{:S(2)}) %collective-permute-start.34) | collective-permute-done | bytes 1048608 | tf_op jit(solution)/shard_map/ppermute | solution.py:95
  591.2 10.1 %collective-permute-done.15 = f32[4,256,512]{2,1,0:T(8,128)} collective-permute-done((f32[4,256,512]{2,1,0:T(8,128)}, f32[4,256,512]{2,1,0:T(8,128)}, u32[]{:S(2)}, u32[]{:S(2)}) %collective-permute-start.15) | collective-permute-done | bytes 2097184 | tf_op jit(solution)/shard_map/ppermute | solution.py:114
  601.3 4.4 fusion.40
  605.9 2.7 collective-permute-done.40
  608.6 3.9 fusion.30
  613.4 4.4 copy.61
  (175 shorter events, 94.6 us)
Async XLA Ops:
  0.0 68.8 %copy-start = (s32[128,128]{1,0:T(8,128)S(1)}, s32[128,128]{1,0:T(8,128)}, u32[]{:S(2)}) copy-start(s32[128,128]{1,0:T(8,128)} %param.7) | copy-start | bytes 196612
  4.8 68.3 %collective-permute-start.16 = (bf16[4,256,512]{2,1,0:T(8,128)(2,1)S(1)}, bf16[4,256,512]{2,1,0:T(8,128)(2,1)}, u32[]{:S(2)}, u32[]{:S(2)}) collective-permute-start(bf16[4,256,512]{2,1,0:T(8,128)(2,1)S(1)} %get-tuple-element.28), channel_id=1, source_target_pairs={{0,1},{1,0},{2,3},{3,2},{4,5},{5,4},{6,7},{7,6},{8,9},{9,8},{10,11... | collective-permute-start | bytes 3145736 | tf_op jit(solution)/shard_map/ppermute | solution.py:17
  5.4 68.2 %collective-permute-start = (bf16[4,256,512]{2,1,0:T(8,128)(2,1)S(1)}, bf16[4,256,512]{2,1,0:T(8,128)(2,1)}, u32[]{:S(2)}, u32[]{:S(2)}) collective-permute-start(bf16[4,256,512]{2,1,0:T(8,128)(2,1)S(1)} %get-tuple-element.30), channel_id=1, source_target_pairs={{0,1},{1,0},{2,3},{3,2},{4,5},{5,4},{6,7},{7,6},{8,9},{9,8},{10,11... | collective-permute-start | bytes 3145736 | tf_op jit(solution)/shard_map/ppermute | solution.py:17
  6.0 84.0 %collective-permute-start.18 = (bf16[4,256,512]{2,1,0:T(8,128)(2,1)S(1)}, bf16[4,256,512]{2,1,0:T(8,128)(2,1)S(1)}, u32[]{:S(2)}, u32[]{:S(2)}) collective-permute-start(bf16[4,256,512]{2,1,0:T(8,128)(2,1)S(1)} %get-tuple-element.28), channel_id=1, source_target_pairs={{2,0},{3,1},{4,2},{5,3},{6,4},{7,5},{10,8},{11,9},{12,10},{13,11},... | collective-permute-start | bytes 3145736 | tf_op jit(solution)/shard_map/ppermute | solution.py:47
  8.4 82.9 %collective-permute-start.10 = (bf16[4,256,512]{2,1,0:T(8,128)(2,1)S(1)}, bf16[4,256,512]{2,1,0:T(8,128)(2,1)}, u32[]{:S(2)}, u32[]{:S(2)}) collective-permute-start(bf16[4,256,512]{2,1,0:T(8,128)(2,1)S(1)} %get-tuple-element.30), channel_id=1, source_target_pairs={{0,8},{8,0},{16,24},{24,16},{1,9},{9,1},{17,25},{25,17},{2,10},{10... | collective-permute-start | bytes 3145736 | tf_op jit(solution)/shard_map/ppermute | solution.py:62
  10.0 82.6 %collective-permute-start.11 = (bf16[4,256,512]{2,1,0:T(8,128)(2,1)S(1)}, bf16[4,256,512]{2,1,0:T(8,128)(2,1)}, u32[]{:S(2)}, u32[]{:S(2)}) collective-permute-start(bf16[4,256,512]{2,1,0:T(8,128)(2,1)S(1)} %get-tuple-element.30), channel_id=1, source_target_pairs={{0,16},{8,24},{16,0},{24,8},{1,17},{9,25},{17,1},{25,9},{2,18},{10... | collective-permute-start | bytes 3145736 | tf_op jit(solution)/shard_map/ppermute | solution.py:62
  11.5 57.2 %copy-start.25 = (s32[8192]{0:T(1024)S(1)}, s32[8192]{0:T(1024)}, u32[]{:S(2)}) copy-start(s32[8192]{0:T(1024)} %param.6) | copy-start | bytes 98308
  73.1 71.1 %copy-start.19 = (bf16[1,512,512]{1,2,0:T(8,128)(2,1)}, bf16[1,512,512]{1,2,0:T(8,128)(2,1)S(1)}, u32[]{:S(2)}) copy-start(bf16[1,512,512]{1,2,0:T(8,128)(2,1)S(1)} %get-tuple-element.68) | copy-start | bytes 1572868
  73.1 71.1 %copy-start.23 = (bf16[1,512,512]{1,2,0:T(8,128)(2,1)}, bf16[1,512,512]{1,2,0:T(8,128)(2,1)S(1)}, u32[]{:S(2)}) copy-start(bf16[1,512,512]{1,2,0:T(8,128)(2,1)S(1)} %get-tuple-element.69) | copy-start | bytes 1572868
  73.1 24.8 %collective-permute-start.28 = (bf16[4,256,512]{2,1,0:T(8,128)(2,1)S(1)}, bf16[4,256,512]{2,1,0:T(8,128)(2,1)}, u32[]{:S(2)}, u32[]{:S(2)}) collective-permute-start(bf16[4,256,512]{2,1,0:T(8,128)(2,1)S(1)} %get-tuple-element.28), channel_id=1, source_target_pairs={{0,16},{8,24},{16,0},{24,8},{1,17},{9,25},{17,1},{25,9},{2,18},{10... | collective-permute-start | bytes 3145736 | tf_op jit(solution)/shard_map/ppermute | solution.py:62
  73.6 25.9 %collective-permute-start.29 = (bf16[4,256,512]{2,1,0:T(8,128)(2,1)S(1)}, bf16[4,256,512]{2,1,0:T(8,128)(2,1)S(1)}, u32[]{:S(2)}, u32[]{:S(2)}) collective-permute-start(bf16[4,256,512]{2,1,0:T(8,128)(2,1)S(1)} %get-tuple-element.28), channel_id=1, source_target_pairs={{0,8},{8,0},{16,24},{24,16},{1,9},{9,1},{17,25},{25,17},{2,10},{10... | collective-permute-start | bytes 3145736 | tf_op jit(solution)/shard_map/ppermute | solution.py:62
  90.0 28.1 %collective-permute-start.17 = (bf16[4,256,512]{2,1,0:T(8,128)(2,1)S(1)}, bf16[4,256,512]{2,1,0:T(8,128)(2,1)}, u32[]{:S(2)}, u32[]{:S(2)}) collective-permute-start(bf16[4,256,512]{2,1,0:T(8,128)(2,1)S(1)} %get-tuple-element.28), channel_id=1, source_target_pairs={{0,2},{1,3},{2,4},{3,5},{4,6},{5,7},{8,10},{9,11},{10,12},{11,13},... | collective-permute-start | bytes 3145736 | tf_op jit(solution)/shard_map/ppermute | solution.py:46
  91.3 46.9 %collective-permute-start.1 = (bf16[4,256,512]{2,1,0:T(8,128)(2,1)S(1)}, bf16[4,256,512]{2,1,0:T(8,128)(2,1)}, u32[]{:S(2)}, u32[]{:S(2)}) collective-permute-start(bf16[4,256,512]{2,1,0:T(8,128)(2,1)S(1)} %get-tuple-element.30), channel_id=1, source_target_pairs={{0,2},{1,3},{2,4},{3,5},{4,6},{5,7},{8,10},{9,11},{10,12},{11,13},... | collective-permute-start | bytes 3145736 | tf_op jit(solution)/shard_map/ppermute | solution.py:46
  92.6 46.8 %collective-permute-start.2 = (bf16[4,256,512]{2,1,0:T(8,128)(2,1)S(1)}, bf16[4,256,512]{2,1,0:T(8,128)(2,1)S(1)}, u32[]{:S(2)}, u32[]{:S(2)}) collective-permute-start(bf16[4,256,512]{2,1,0:T(8,128)(2,1)S(1)} %get-tuple-element.30), channel_id=1, source_target_pairs={{2,0},{3,1},{4,2},{5,3},{6,4},{7,5},{10,8},{11,9},{12,10},{13,11},... | collective-permute-start | bytes 3145736 | tf_op jit(solution)/shard_map/ppermute | solution.py:47
  97.9 43.3 %collective-permute-start.19 = (bf16[4,256,512]{2,1,0:T(8,128)(2,1)S(1)}, bf16[4,256,512]{2,1,0:T(8,128)(2,1)}, u32[]{:S(2)}, u32[]{:S(2)}) collective-permute-start(bf16[4,256,512]{2,1,0:T(8,128)(2,1)S(1)} %collective-permute-done.18), channel_id=1, source_target_pairs={{2,0},{3,1},{4,2},{5,3},{10,8},{11,9},{12,10},{13,11},{18,16},{19,... | collective-permute-start | bytes 3145736 | tf_op jit(solution)/shard_map/ppermute | solution.py:47
  99.5 42.9 %collective-permute-start.12 = (bf16[4,256,512]{2,1,0:T(8,128)(2,1)}, bf16[4,256,512]{2,1,0:T(8,128)(2,1)S(1)}, u32[]{:S(2)}, u32[]{:S(2)}) collective-permute-start(bf16[4,256,512]{2,1,0:T(8,128)(2,1)} %collective-permute-done.10), channel_id=1, source_target_pairs={{0,16},{8,24},{16,0},{24,8},{1,17},{9,25},{17,1},{25,9},{2,18},{10... | collective-permute-start | bytes 3145736 | tf_op jit(solution)/shard_map/ppermute | solution.py:62
  118.1 82.2 %collective-permute-start.30 = (bf16[4,256,512]{2,1,0:T(8,128)(2,1)}, bf16[4,256,512]{2,1,0:T(8,128)(2,1)}, u32[]{:S(2)}, u32[]{:S(2)}) collective-permute-start(bf16[4,256,512]{2,1,0:T(8,128)(2,1)} %collective-permute-done.28), channel_id=1, source_target_pairs={{0,8},{8,0},{16,24},{24,16},{1,9},{9,1},{17,25},{25,17},{2,10},{10... | collective-permute-start | bytes 3145736 | tf_op jit(solution)/shard_map/ppermute | solution.py:62
  138.2 60.8 %collective-permute-start.22 = (bf16[4,256,512]{2,1,0:T(8,128)(2,1)}, bf16[4,256,512]{2,1,0:T(8,128)(2,1)}, u32[]{:S(2)}, u32[]{:S(2)}) collective-permute-start(bf16[4,256,512]{2,1,0:T(8,128)(2,1)} %collective-permute-done.17), channel_id=1, source_target_pairs={{2,4},{3,5},{4,6},{5,7},{10,12},{11,13},{12,14},{13,15},{18,20},{1... | collective-permute-start | bytes 3145736 | tf_op jit(solution)/shard_map/ppermute | solution.py:46
  139.5 11.6 %collective-permute-start.3 = (bf16[4,256,512]{2,1,0:T(8,128)(2,1)S(1)}, bf16[4,256,512]{2,1,0:T(8,128)(2,1)}, u32[]{:S(2)}, u32[]{:S(2)}) collective-permute-start(bf16[4,256,512]{2,1,0:T(8,128)(2,1)S(1)} %collective-permute-done.2), channel_id=1, source_target_pairs={{2,0},{3,1},{4,2},{5,3},{10,8},{11,9},{12,10},{13,11},{18,16},{19,... | collective-permute-start | bytes 3145736 | tf_op jit(solution)/shard_map/ppermute | solution.py:47
  141.1 57.9 %collective-permute-start.6 = (bf16[4,256,512]{2,1,0:T(8,128)(2,1)}, bf16[4,256,512]{2,1,0:T(8,128)(2,1)}, u32[]{:S(2)}, u32[]{:S(2)}) collective-permute-start(bf16[4,256,512]{2,1,0:T(8,128)(2,1)} %collective-permute-done.1), channel_id=1, source_target_pairs={{2,4},{3,5},{4,6},{5,7},{10,12},{11,13},{12,14},{13,15},{18,20},{1... | collective-permute-start | bytes 3145736 | tf_op jit(solution)/shard_map/ppermute | solution.py:46
  142.4 37.0 %collective-permute-start.20 = (bf16[4,256,512]{2,1,0:T(8,128)(2,1)}, bf16[4,256,512]{2,1,0:T(8,128)(2,1)}, u32[]{:S(2)}, u32[]{:S(2)}) collective-permute-start(bf16[4,256,512]{2,1,0:T(8,128)(2,1)} %collective-permute-done.19), channel_id=1, source_target_pairs={{2,0},{3,1},{10,8},{11,9},{18,16},{19,17},{26,24},{27,25}} | collective-permute-start | bytes 3145736 | tf_op jit(solution)/shard_map/ppermute | solution.py:47
  151.0 30.9 %collective-permute-start.4 = (bf16[4,256,512]{2,1,0:T(8,128)(2,1)}, bf16[4,256,512]{2,1,0:T(8,128)(2,1)}, u32[]{:S(2)}, u32[]{:S(2)}) collective-permute-start(bf16[4,256,512]{2,1,0:T(8,128)(2,1)} %collective-permute-done.3), channel_id=1, source_target_pairs={{2,0},{3,1},{10,8},{11,9},{18,16},{19,17},{26,24},{27,25}} | collective-permute-start | bytes 3145736 | tf_op jit(solution)/shard_map/ppermute | solution.py:47
  182.0 21.4 %collective-permute-start.21 = (bf16[4,256,512]{2,1,0:T(8,128)(2,1)S(1)}, bf16[4,256,512]{2,1,0:T(8,128)(2,1)S(1)}, u32[]{:S(2)}, u32[]{:S(2)}) collective-permute-start(bf16[4,256,512]{2,1,0:T(8,128)(2,1)S(1)} %get-tuple-element.42), channel_id=1, source_target_pairs={{0,1},{1,0},{2,3},{3,2},{4,5},{5,4},{6,7},{7,6},{8,9},{9,8},{10,11... | collective-permute-start | bytes 3145736 | tf_op jit(solution)/shard_map/ppermute | solution.py:17
  184.5 22.9 %collective-permute-start.5 = (bf16[4,256,512]{2,1,0:T(8,128)(2,1)S(1)}, bf16[4,256,512]{2,1,0:T(8,128)(2,1)S(1)}, u32[]{:S(2)}, u32[]{:S(2)}) collective-permute-start(bf16[4,256,512]{2,1,0:T(8,128)(2,1)S(1)} %get-tuple-element.36), channel_id=1, source_target_pairs={{0,1},{1,0},{2,3},{3,2},{4,5},{5,4},{6,7},{7,6},{8,9},{9,8},{10,11... | collective-permute-start | bytes 3145736 | tf_op jit(solution)/shard_map/ppermute | solution.py:17
  199.0 108.9 %collective-permute-start.13 = (f32[4,4,256,512]{3,2,0,1:T(8,128)}, f32[4,4,256,512]{3,2,0,1:T(8,128)}, u32[]{:S(2)}, u32[]{:S(2)}) collective-permute-start(f32[4,4,256,512]{3,2,0,1:T(8,128)} %bitcast.316), channel_id=1, source_target_pairs={{0,1},{1,0},{2,3},{3,2},{4,5},{5,4},{6,7},{7,6},{8,9},{9,8},{10,11... | collective-permute-start | bytes 25165832 | tf_op jit(solution)/shard_map/ppermute | solution.py:17
  199.0 39.9 %collective-permute-start.24 = (bf16[4,256,512]{2,1,0:T(8,128)(2,1)}, bf16[4,256,512]{2,1,0:T(8,128)(2,1)S(1)}, u32[]{:S(2)}, u32[]{:S(2)}) collective-permute-start(bf16[4,256,512]{2,1,0:T(8,128)(2,1)} %collective-permute-done.22), channel_id=1, source_target_pairs={{4,6},{5,7},{12,14},{13,15},{20,22},{21,23},{28,30},{29,31}} | collective-permute-start | bytes 3145736 | tf_op jit(solution)/shard_map/ppermute | solution.py:46
  200.3 60.9 %collective-permute-start.8 = (bf16[4,256,512]{2,1,0:T(8,128)(2,1)}, bf16[4,256,512]{2,1,0:T(8,128)(2,1)S(1)}, u32[]{:S(2)}, u32[]{:S(2)}) collective-permute-start(bf16[4,256,512]{2,1,0:T(8,128)(2,1)} %collective-permute-done.6), channel_id=1, source_target_pairs={{4,6},{5,7},{12,14},{13,15},{20,22},{21,23},{28,30},{29,31}} | collective-permute-start | bytes 3145736 | tf_op jit(solution)/shard_map/ppermute | solution.py:46
  207.0 11.0 %collective-permute-start.23 = (bf16[4,256,512]{2,1,0:T(8,128)(2,1)S(1)}, bf16[4,256,512]{2,1,0:T(8,128)(2,1)S(1)}, u32[]{:S(2)}, u32[]{:S(2)}) collective-permute-start(bf16[4,256,512]{2,1,0:T(8,128)(2,1)S(1)} %get-tuple-element.40), channel_id=1, source_target_pairs={{0,1},{1,0},{2,3},{3,2},{4,5},{5,4},{6,7},{7,6},{8,9},{9,8},{10,11... | collective-permute-start | bytes 3145736 | tf_op jit(solution)/shard_map/ppermute | solution.py:17
  211.0 29.5 %collective-permute-start.7 = (bf16[4,256,512]{2,1,0:T(8,128)(2,1)S(1)}, bf16[4,256,512]{2,1,0:T(8,128)(2,1)S(1)}, u32[]{:S(2)}, u32[]{:S(2)}) collective-permute-start(bf16[4,256,512]{2,1,0:T(8,128)(2,1)S(1)} %get-tuple-element.34), channel_id=1, source_target_pairs={{0,1},{1,0},{2,3},{3,2},{4,5},{5,4},{6,7},{7,6},{8,9},{9,8},{10,11... | collective-permute-start | bytes 3145736 | tf_op jit(solution)/shard_map/ppermute | solution.py:17
  240.5 62.8 %collective-permute-start.25 = (bf16[4,256,512]{2,1,0:T(8,128)(2,1)}, bf16[4,256,512]{2,1,0:T(8,128)(2,1)}, u32[]{:S(2)}, u32[]{:S(2)}) collective-permute-start(bf16[4,256,512]{2,1,0:T(8,128)(2,1)} %get-tuple-element.38), channel_id=1, source_target_pairs={{0,1},{1,0},{2,3},{3,2},{4,5},{5,4},{6,7},{7,6},{8,9},{9,8},{10,11... | collective-permute-start | bytes 3145736 | tf_op jit(solution)/shard_map/ppermute | solution.py:17
  262.5 43.1 %collective-permute-start.9 = (bf16[4,256,512]{2,1,0:T(8,128)(2,1)S(1)}, bf16[4,256,512]{2,1,0:T(8,128)(2,1)}, u32[]{:S(2)}, u32[]{:S(2)}) collective-permute-start(bf16[4,256,512]{2,1,0:T(8,128)(2,1)S(1)} %get-tuple-element.32), channel_id=1, source_target_pairs={{0,1},{1,0},{2,3},{3,2},{4,5},{5,4},{6,7},{7,6},{8,9},{9,8},{10,11... | collective-permute-start | bytes 3145736 | tf_op jit(solution)/shard_map/ppermute | solution.py:17
  302.8 79.8 %collective-permute-start.31 = (f32[4,4,256,512]{3,2,0,1:T(8,128)}, f32[4,4,256,512]{3,2,0,1:T(8,128)}, u32[]{:S(2)}, u32[]{:S(2)}) collective-permute-start(f32[4,4,256,512]{3,2,0,1:T(8,128)} %bitcast.315), channel_id=1, source_target_pairs={{0,1},{1,0},{2,3},{3,2},{4,5},{5,4},{6,7},{7,6},{8,9},{9,8},{10,11... | collective-permute-start | bytes 25165832 | tf_op jit(solution)/shard_map/ppermute | solution.py:17
  323.7 74.7 %collective-permute-start.27 = (f16[4,256,512]{2,1,0:T(8,128)(2,1)}, f16[4,256,512]{2,1,0:T(8,128)(2,1)S(1)}, u32[]{:S(2)}, u32[]{:S(2)}) collective-permute-start(f16[4,256,512]{2,1,0:T(8,128)(2,1)} %get-tuple-element.18), channel_id=1, source_target_pairs={{6,4},{7,5},{14,12},{15,13},{22,20},{23,21},{30,28},{31,29}} | collective-permute-start | bytes 3145736 | tf_op jit(solution)/shard_map/ppermute | solution.py:96
  325.3 73.1 %collective-permute-start.26 = (f16[4,256,512]{2,1,0:T(8,128)(2,1)}, f16[4,256,512]{2,1,0:T(8,128)(2,1)}, u32[]{:S(2)}, u32[]{:S(2)}) collective-permute-start(f16[4,256,512]{2,1,0:T(8,128)(2,1)} %get-tuple-element.17), channel_id=1, source_target_pairs={{0,2},{1,3},{8,10},{9,11},{16,18},{17,19},{24,26},{25,27}} | collective-permute-start | bytes 3145736 | tf_op jit(solution)/shard_map/ppermute | solution.py:95
  381.2 146.4 %collective-permute-start.14 = (f32[4,2,256,512]{3,2,0,1:T(8,128)}, f32[4,2,256,512]{3,2,0,1:T(8,128)}, u32[]{:S(2)}, u32[]{:S(2)}) collective-permute-start(f32[4,2,256,512]{3,2,0,1:T(8,128)} %bitcast.318), channel_id=1, source_target_pairs={{0,8},{8,0},{16,24},{24,16},{1,9},{9,1},{17,25},{25,17},{2,10},{10... | collective-permute-start | bytes 12582920 | tf_op jit(solution)/shard_map/ppermute | solution.py:114
  402.8 18.9 %collective-permute-start.32 = (f16[4,256,512]{2,1,0:T(8,128)(2,1)S(1)}, f16[4,256,512]{2,1,0:T(8,128)(2,1)}, u32[]{:S(2)}, u32[]{:S(2)}) collective-permute-start(f16[4,256,512]{2,1,0:T(8,128)(2,1)S(1)} %get-tuple-element.20), channel_id=1, source_target_pairs={{0,2},{1,3},{2,4},{3,5},{8,10},{9,11},{10,12},{11,13},{16,18},{17,... | collective-permute-start | bytes 3145736 | tf_op jit(solution)/shard_map/ppermute | solution.py:95
  404.5 23.9 %collective-permute-start.33 = (f16[4,256,512]{2,1,0:T(8,128)(2,1)}, f16[4,256,512]{2,1,0:T(8,128)(2,1)S(1)}, u32[]{:S(2)}, u32[]{:S(2)}) collective-permute-start(f16[4,256,512]{2,1,0:T(8,128)(2,1)} %get-tuple-element.21), channel_id=1, source_target_pairs={{4,2},{5,3},{6,4},{7,5},{12,10},{13,11},{14,12},{15,13},{20,18},{2... | collective-permute-start | bytes 3145736 | tf_op jit(solution)/shard_map/ppermute | solution.py:96
  464.7 93.8 %collective-permute-start.36 = (f32[4,2,256,512]{3,2,0,1:T(8,128)}, f32[4,2,256,512]{3,2,0,1:T(8,128)}, u32[]{:S(2)}, u32[]{:S(2)}) collective-permute-start(f32[4,2,256,512]{3,2,0,1:T(8,128)} %bitcast.317), channel_id=1, source_target_pairs={{0,16},{8,24},{16,0},{24,8},{1,17},{9,25},{17,1},{25,9},{2,18},{10... | collective-permute-start | bytes 12582920 | tf_op jit(solution)/shard_map/ppermute | solution.py:114
  466.2 5.1 collective-permute-start.38
  466.9 28.2 %collective-permute-start.41 = (f16[4,256,512]{2,1,0:T(8,128)(2,1)}, f16[4,256,512]{2,1,0:T(8,128)(2,1)S(1)}, u32[]{:S(2)}, u32[]{:S(2)}) collective-permute-start(f16[4,256,512]{2,1,0:T(8,128)(2,1)} %get-tuple-element.26), channel_id=1, source_target_pairs={{6,4},{7,5},{14,12},{15,13},{22,20},{23,21},{30,28},{31,29}} | collective-permute-start | bytes 3145736 | tf_op jit(solution)/shard_map/ppermute | solution.py:96
  474.3 21.7 %collective-permute-start.39 = (f16[4,256,512]{2,1,0:T(8,128)(2,1)}, f16[4,256,512]{2,1,0:T(8,128)(2,1)}, u32[]{:S(2)}, u32[]{:S(2)}) collective-permute-start(f16[4,256,512]{2,1,0:T(8,128)(2,1)} %fusion.26), channel_id=1, source_target_pairs={{0,2},{1,3},{2,4},{3,5},{8,10},{9,11},{10,12},{11,13},{16,18},{17,... | collective-permute-start | bytes 3145736 | tf_op jit(solution)/shard_map/ppermute | solution.py:95
  480.9 87.2 %collective-permute-start.35 = (f16[4,256,512]{2,1,0:T(8,128)(2,1)S(1)}, f16[4,256,512]{2,1,0:T(8,128)(2,1)S(1)}, u32[]{:S(2)}, u32[]{:S(2)}) collective-permute-start(f16[4,256,512]{2,1,0:T(8,128)(2,1)S(1)} %get-tuple-element.48), channel_id=1, source_target_pairs={{2,0},{3,1},{4,2},{5,3},{6,4},{7,5},{10,8},{11,9},{12,10},{13,11},... | collective-permute-start | bytes 3145736 | tf_op jit(solution)/shard_map/ppermute | solution.py:96
  499.7 64.0 %collective-permute-start.42 = (f16[4,256,512]{2,1,0:T(8,128)(2,1)S(1)}, f16[4,256,512]{2,1,0:T(8,128)(2,1)S(1)}, u32[]{:S(2)}, u32[]{:S(2)}) collective-permute-start(f16[4,256,512]{2,1,0:T(8,128)(2,1)S(1)} %get-tuple-element.52), channel_id=1, source_target_pairs={{4,2},{5,3},{6,4},{7,5},{12,10},{13,11},{14,12},{15,13},{20,18},{2... | collective-permute-start | bytes 3145736 | tf_op jit(solution)/shard_map/ppermute | solution.py:96
  532.4 68.9 %collective-permute-start.15 = (f32[4,256,512]{2,1,0:T(8,128)}, f32[4,256,512]{2,1,0:T(8,128)}, u32[]{:S(2)}, u32[]{:S(2)}) collective-permute-start(f32[4,256,512]{2,1,0:T(8,128)} %dynamic-slice_bitcast_fusion.1), channel_id=1, source_target_pairs={{0,16},{8,24},{16,0},{24,8},{1,17},{9,25},{17,1},{25,9},{2,18},{10... | collective-permute-start | bytes 6291464 | tf_op jit(solution)/shard_map/ppermute | solution.py:114
  561.9 46.7 %collective-permute-start.37 = (f32[4,256,512]{2,1,0:T(8,128)S(1)}, f32[4,256,512]{2,1,0:T(8,128)}, u32[]{:S(2)}, u32[]{:S(2)}) collective-permute-start(f32[4,256,512]{2,1,0:T(8,128)S(1)} %dynamic-slice_bitcast_fusion), channel_id=1, source_target_pairs={{0,8},{8,0},{16,24},{24,16},{1,9},{9,1},{17,25},{25,17},{2,10},{10... | collective-permute-start | bytes 6291464 | tf_op jit(solution)/shard_map/ppermute | solution.py:114
  562.5 28.7 %collective-permute-start.34 = (f16[4,256,512]{2,1,0:T(8,128)(2,1)}, f16[4,256,512]{2,1,0:T(8,128)(2,1)}, u32[]{:S(2)}, u32[]{:S(2)}) collective-permute-start(f16[4,256,512]{2,1,0:T(8,128)(2,1)} %get-tuple-element.47), channel_id=1, source_target_pairs={{0,2},{1,3},{2,4},{3,5},{4,6},{5,7},{8,10},{9,11},{10,12},{11,13},... | collective-permute-start | bytes 3145736 | tf_op jit(solution)/shard_map/ppermute | solution.py:95
  563.8 44.8 %collective-permute-start.40 = (f16[4,256,512]{2,1,0:T(8,128)(2,1)S(1)}, f16[4,256,512]{2,1,0:T(8,128)(2,1)}, u32[]{:S(2)}, u32[]{:S(2)}) collective-permute-start(f16[4,256,512]{2,1,0:T(8,128)(2,1)S(1)} %get-tuple-element.51), channel_id=1, source_target_pairs={{0,2},{1,3},{2,4},{3,5},{4,6},{5,7},{8,10},{9,11},{10,12},{11,13},... | collective-permute-start | bytes 3145736 | tf_op jit(solution)/shard_map/ppermute | solution.py:95
  569.1 39.5 %collective-permute-start.43 = (f16[4,256,512]{2,1,0:T(8,128)(2,1)}, f16[4,256,512]{2,1,0:T(8,128)(2,1)}, u32[]{:S(2)}, u32[]{:S(2)}) collective-permute-start(f16[4,256,512]{2,1,0:T(8,128)(2,1)} %fusion.24), channel_id=1, source_target_pairs={{2,0},{3,1},{4,2},{5,3},{6,4},{7,5},{10,8},{11,9},{12,10},{13,11},... | collective-permute-start | bytes 3145736 | tf_op jit(solution)/shard_map/ppermute | solution.py:96
  (22 other events, 253.6 us)
